TPU v7x, 32 devices: a whole 2x2x4 slice. The times are simulated.
32 devices in a mesh: grp: 2 (over x), chol: 16 (over z, y, core).
Axes of the slice: x: 2, y: 2, z: 4, core: 2. Of those that a mesh axis runs over, the one named last changes fastest.
Arguments:
- chol_full: bfloat16 [128, 1024, 1024], P(None, 'chol'), may hold values from -0.015625 to 0.015625
- chol_half: bfloat16 [128, 1024, 256], P(None, 'chol'), may hold values from -0.046875 to 0.046875
- green: bfloat16 [128, 1024, 256], P('grp', 'chol'), parts along dimension 0, may hold values from -6 to 6
- gauss: float32 [128, 128], P('grp'), parts along dimension 0, may hold values from -5 to 5
- orbitals: bfloat16 [128, 1024, 256], P(('grp', 'chol')), parts along dimension 0, may hold values from -6 to 6
Outputs:
- new_orbitals: bfloat16 [128, 1024, 256], P(('grp', 'chol')), parts along dimension 0
- log_factor: float32 [128], P(('grp', 'chol')), parts along dimension 0
There are 2 independent parts, one for each index of `grp`. A program takes and returns all parts, laid end to end along the dimension named above; an argument that names none is the same for every part. Nothing has to cross between parts.
All inputs are finite; a program needn't handle non-finite values.
Results may differ from a plain program's by a relative error of at most 0.0032.
Values may be sent and summed in bfloat16 or wider, within the bound.
A program may use at most 128 MiB of HBM per device.

v0:
```python
import functools

import jax
import jax.numpy as jnp
from jax import lax
from jax.experimental import pallas as pl
from jax.experimental.pallas import tpu as pltpu
from jax.sharding import PartitionSpec as P

TILE = 16
LANES = 128
PLANE = 4
GUEST_LIMIT = 16 << 20


def remote(src, dst, send, recv, peer):
    return pltpu.make_async_remote_copy(
        src_ref=src,
        dst_ref=dst,
        send_sem=send,
        recv_sem=recv,
        device_id={"chol": peer},
        device_id_type=pl.DeviceIdType.MESH,
    )


def direct_kernel(
    n, chol_hbm, half_hbm, green_hbm, gauss_ref, orb_ref,
    out_ref, log_ref,
    chol, half, green, part, part_in, fields_own, fields_in, send, recv,
    load_sem, aux_sem, part_send, part_recv, field_send, field_recv, pot_send, pot_recv,
):
    me = lax.axis_index("chol")
    owned = part.shape[1]
    tiles = chol.shape[0]
    width = chol.shape[3]

    half_copy = pltpu.make_async_copy(half_hbm, half, aux_sem.at[0])
    green_copy = pltpu.make_async_copy(green_hbm, green, aux_sem.at[1])
    half_copy.start()
    green_copy.start()
    loads = [
        pltpu.make_async_copy(chol_hbm.at[:, pl.ds(t * TILE, TILE), :], chol.at[t], load_sem.at[t])
        for t in range(tiles)
    ]
    for load in loads:
        load.start()

    barrier = pltpu.get_barrier_semaphore()

    def greet(k, _):
        pl.semaphore_signal(
            barrier, inc=1, device_id={"chol": lax.rem(me + k, n)}, device_id_type=pl.DeviceIdType.MESH
        )
        return 0

    lax.fori_loop(1, n, greet, 0)

    half_copy.wait()
    green_copy.wait()

    def bias(t, acc):
        rows = pl.ds(pl.multiple_of(t * TILE, TILE), TILE)
        left = jnp.swapaxes(green[:, rows, :], 0, 1)
        right = jnp.swapaxes(half[:, rows, :], 0, 1)
        for r in range(TILE):
            acc += lax.dot_general(
                left[r], right[r], (((1,), (1,)), ((), ())), preferred_element_type=jnp.float32
            )
        return acc

    total = lax.fori_loop(0, tiles, bias, jnp.zeros((n * owned, half.shape[0]), jnp.float32))
    for d in range(n):
        part[d] = total[d * owned:(d + 1) * owned]
    pl.semaphore_wait(barrier, n - 1)

    def peer_of(k):
        return lax.rem(me + k, n)

    def push_part(k, _):
        to = peer_of(k)
        remote(part.at[to], part_in.at[me], part_send.at[to], part_recv.at[me], to).start()
        return 0

    lax.fori_loop(1, n, push_part, 0)
    part_in[me] = part[me]

    def wait_part(k, _):
        peer = peer_of(k)
        copy = remote(part.at[peer], part_in.at[peer], part_send.at[peer], part_recv.at[peer], peer)
        copy.wait_recv()
        return 0

    lax.fori_loop(1, n, wait_part, 0)
    vbias = jnp.sum(part_in[...], axis=0)
    gauss = gauss_ref[me]
    xbar = jnp.clip(-0.3 * vbias, -1.0, 1.0)
    log_ref[...] = jnp.broadcast_to(
        jnp.sum(gauss * xbar - 0.5 * xbar * xbar, axis=1, keepdims=True), log_ref.shape
    )
    mine = gauss - xbar
    fields_own[...] = mine
    fields_in[me] = mine

    def push_field(k, _):
        to = peer_of(k)
        remote(fields_own, fields_in.at[me], field_send.at[to], field_recv.at[me], to).start()
        return 0

    lax.fori_loop(1, n, push_field, 0)

    def wait_field(k, _):
        peer = peer_of(k)
        remote(fields_own, fields_in.at[peer], field_send.at[peer], field_recv.at[peer], peer).wait_recv()
        return 0

    lax.fori_loop(1, n, wait_field, 0)
    fields = jnp.concatenate([fields_in[d] for d in range(n)], axis=0).astype(jnp.bfloat16)

    def walkers_of(d):
        return pl.ds(d * owned, owned)

    def rows_of(d):
        return pl.ds(pl.multiple_of(d * TILE, TILE), TILE)

    for t in range(tiles):
        loads[t].wait()

        def strip(c, _):
            cols = pl.ds(pl.multiple_of(c * LANES, LANES), LANES)
            block = jnp.swapaxes(chol[t, :, :, cols], 0, 1)
            pots = [
                (jnp.dot(fields, block[r], preferred_element_type=jnp.float32) * 0.3).astype(jnp.bfloat16)
                for r in range(TILE)
            ]
            send[t, :, :, cols] = jnp.swapaxes(jnp.stack(pots, axis=0), 0, 1)
            return 0

        lax.fori_loop(0, width // LANES, strip, 0)

        def push_pot(k, _):
            to = peer_of(k)
            remote(
                send.at[t, walkers_of(to)], recv.at[t, :, rows_of(me), :],
                pot_send.at[t, to], pot_recv.at[t, me], to,
            ).start()
            return 0

        lax.fori_loop(1, n, push_pot, 0)
        recv[t, :, rows_of(me), :] = send[t, walkers_of(me)]

    for t in range(tiles):

        def wait_pot(k, _):
            peer = peer_of(k)
            remote(
                send.at[t, walkers_of(peer)], recv.at[t, :, rows_of(peer), :],
                pot_send.at[t, peer], pot_recv.at[t, peer], peer,
            ).wait_recv()
            return 0

        lax.fori_loop(1, n, wait_pot, 0)

        def advance(w, _):
            orbit = orb_ref[w].reshape(width, orb_ref.shape[-1])
            for first in range(0, n, 16):
                span = min(16, n - first)
                moved = jnp.dot(
                    recv[t, w, first * TILE:(first + span) * TILE, :], orbit,
                    preferred_element_type=jnp.float32,
                ).reshape(span, TILE, orbit.shape[-1])
                old = orb_ref[w, first:first + span, t].astype(jnp.float32)
                out_ref[w, first:first + span, t] = (old + moved).astype(jnp.bfloat16)
            return 0

        lax.fori_loop(0, owned, advance, 0)

    def drain(k, _):
        peer = peer_of(k)
        remote(part.at[peer], part_in.at[peer], part_send.at[peer], part_recv.at[peer], peer).wait_send()
        remote(fields_own, fields_in.at[peer], field_send.at[peer], field_recv.at[peer], peer).wait_send()
        for t in range(tiles):
            remote(
                send.at[t, walkers_of(peer)], recv.at[t, :, rows_of(peer), :],
                pot_send.at[t, peer], pot_recv.at[t, peer], peer,
            ).wait_send()
        return 0

    lax.fori_loop(1, n, drain, 0)


def relay_kernel(
    n, chol_hbm, half_hbm, green_hbm, gauss_ref, orb_ref,
    out_ref, log_ref,
    chol, half, green, part, part_in, fields_own, fields_in, send, recv, guest, done, hop,
    load_sem, aux_sem, part_send, part_recv, field_send, field_recv, pot_send, pot_recv,
    own_send, guest_recv, relay_send, pass_send, done_send, done_recv, hop_send, hop_recv,
):
    me = lax.axis_index("chol")
    owned = part.shape[1]
    tiles = chol.shape[0]
    width = chol.shape[3]

    half_copy = pltpu.make_async_copy(half_hbm, half, aux_sem.at[0])
    green_copy = pltpu.make_async_copy(green_hbm, green, aux_sem.at[1])
    half_copy.start()
    green_copy.start()
    loads = [
        pltpu.make_async_copy(chol_hbm.at[:, pl.ds(t * TILE, TILE), :], chol.at[t], load_sem.at[t])
        for t in range(tiles)
    ]
    for load in loads:
        load.start()

    barrier = pltpu.get_barrier_semaphore()

    def greet(k, _):
        pl.semaphore_signal(
            barrier, inc=1, device_id={"chol": lax.rem(me + k, n)}, device_id_type=pl.DeviceIdType.MESH
        )
        return 0

    lax.fori_loop(1, n, greet, 0)

    half_copy.wait()
    green_copy.wait()

    def bias(t, acc):
        rows = pl.ds(pl.multiple_of(t * TILE, TILE), TILE)
        left = jnp.swapaxes(green[:, rows, :], 0, 1)
        right = jnp.swapaxes(half[:, rows, :], 0, 1)
        for r in range(TILE):
            acc += lax.dot_general(
                left[r], right[r], (((1,), (1,)), ((), ())), preferred_element_type=jnp.float32
            )
        return acc

    total = lax.fori_loop(0, tiles, bias, jnp.zeros((n * owned, half.shape[0]), jnp.float32))
    for d in range(n):
        part[d] = total[d * owned:(d + 1) * owned]
    pl.semaphore_wait(barrier, n - 1)

    def peer_of(k):
        return lax.rem(me + k, n)

    def push_part(k, _):
        to = peer_of(k)
        remote(part.at[to], part_in.at[me], part_send.at[to], part_recv.at[me], to).start()
        return 0

    lax.fori_loop(1, n, push_part, 0)
    part_in[me] = part[me]

    def wait_part(k, _):
        peer = peer_of(k)
        copy = remote(part.at[peer], part_in.at[peer], part_send.at[peer], part_recv.at[peer], peer)
        copy.wait_recv()
        return 0

    lax.fori_loop(1, n, wait_part, 0)
    vbias = jnp.sum(part_in[...], axis=0)
    gauss = gauss_ref[me]
    xbar = jnp.clip(-0.3 * vbias, -1.0, 1.0)
    log_ref[...] = jnp.broadcast_to(
        jnp.sum(gauss * xbar - 0.5 * xbar * xbar, axis=1, keepdims=True), log_ref.shape
    )
    mine = gauss - xbar
    fields_own[...] = mine
    fields_in[me] = mine

    def push_field(k, _):
        to = peer_of(k)
        remote(fields_own, fields_in.at[me], field_send.at[to], field_recv.at[me], to).start()
        return 0

    lax.fori_loop(1, n, push_field, 0)

    def wait_field(k, _):
        peer = peer_of(k)
        remote(fields_own, fields_in.at[peer], field_send.at[peer], field_recv.at[peer], peer).wait_recv()
        return 0

    lax.fori_loop(1, n, wait_field, 0)
    fields = jnp.concatenate([fields_in[d] for d in range(n)], axis=0).astype(jnp.bfloat16)

    def walkers_of(d):
        return pl.ds(d * owned, owned)

    def rows_of(d):
        return pl.ds(pl.multiple_of(d * TILE, TILE), TILE)

    near = n // 2
    planes = near // PLANE
    mine_at = lax.rem(me, near)
    home = me - mine_at
    away = near - home
    seat = lax.rem(me, PLANE)
    across = lax.rem(seat + 2, PLANE)
    upper = me // near
    entry = away + (1 - upper) * 0 + upper * (near - PLANE) + seat
    depth = upper * (mine_at // PLANE) + (1 - upper) * (planes - 1 - mine_at // PLANE)
    outward = lax.rem(me + n + (2 * upper - 1) * PLANE, n)
    inward = lax.rem(me + n - (2 * upper - 1) * PLANE, n)
    partner = me + 1 - 2 * lax.rem(me, 2)
    beside = me - seat + across

    def swap(j):
        return j + 1 - 2 * lax.rem(j, 2)

    def guest_copy(slot, w, sem, to):
        return remote(guest.at[slot, w], guest.at[slot, w], sem, guest_recv.at[slot, w], to)

    inner = depth == 0
    outer = depth > 0
    behind = lax.rem(outward, near)

    def host(w):
        return remote(orb_ref.at[w], guest.at[mine_at, w], own_send.at[w], guest_recv.at[mine_at, w], entry)

    def lift(w):
        return remote(orb_ref.at[w], hop.at[w], own_send.at[w], hop_recv.at[w], inward)

    def onward(w):
        return remote(hop.at[w], guest.at[behind, w], hop_send.at[w], guest_recv.at[behind, w], entry)

    @pl.when(inner)
    def _():
        for w in range(owned):
            host(w).start()

    @pl.when(outer)
    def _():
        for w in range(owned):
            lift(w).start()

    def forward(w):
        @pl.when(inner)
        def _():
            lift(w).wait_recv()
            onward(w).start()

    def fill(t):
        loads[t].wait()

        def strip(c, _):
            cols = pl.ds(pl.multiple_of(c * LANES, LANES), LANES)
            block = jnp.swapaxes(chol[t, :, :, cols], 0, 1)
            pots = [
                (jnp.dot(fields, block[r], preferred_element_type=jnp.float32) * 0.3).astype(jnp.bfloat16)
                for r in range(TILE)
            ]
            send[t, :, :, cols] = jnp.swapaxes(jnp.stack(pots, axis=0), 0, 1)
            return 0

        lax.fori_loop(0, width // LANES, strip, 0)
        recv[t, :, rows_of(mine_at), :] = send[t, walkers_of(me)]

    def fellow(k):
        return lax.rem(mine_at + k, near)

    def pot_copy(t, there, source):
        return remote(
            send.at[t, walkers_of(home + there)], recv.at[t, :, rows_of(source), :],
            pot_send.at[t, there], pot_recv.at[t, source], home + there,
        )

    def push(t):
        def step(k, _):
            pot_copy(t, fellow(k), mine_at).start()
            return 0

        lax.fori_loop(1, near, step, 0)

    first = away // near

    def block(s):
        oz = s // owned
        return (oz + (1 - 2 * oz) * (1 - first), s % owned)

    def relay(s):
        oz, w = block(s)
        slot = oz * PLANE + seat
        guest_copy(slot, w, own_send.at[w], partner).wait_recv()

        @pl.when(inner)
        def _():
            guest_copy(slot, w, relay_send.at[0, s], outward).start()

        guest_copy(slot, w, relay_send.at[1, s], beside).start()
        guest_copy(slot, w, relay_send.at[2, s], partner).start()

    def hand_over(s):
        oz, w = block(s)
        slot = oz * PLANE + across
        guest_copy(slot, w, own_send.at[w], partner).wait_recv()
        guest_copy(slot, w, pass_send.at[s], partner).start()

    def done_copy(slot, w):
        return remote(
            done.at[slot, w], out_ref.at[w, me], done_send.at[slot, w], done_recv.at[mine_at, w], away + slot
        )

    def serve(slot, w):
        left = send[:, (away + slot) * owned + w].reshape(tiles * TILE, width)
        orbit = guest[slot, w].reshape(width, guest.shape[-1])
        moved = jnp.dot(left, orbit, preferred_element_type=jnp.float32)
        old = guest[slot, w, me].astype(jnp.float32)
        done[slot, w] = (old + moved.reshape(old.shape)).astype(jnp.bfloat16)
        done_copy(slot, w).start()

    def serve_block(s, j, wait):
        oz, w = block(s)
        slot = oz * PLANE + j
        if wait:
            guest_copy(slot, w, own_send.at[w], partner).wait_recv()
        serve(slot, w)

    steps = planes * owned
    early = tiles - 1
    for t in range(tiles):
        fill(t)
        if t < early:
            push(t)
    for s in range(steps + 2):
        if s < owned:
            forward(s)
        if s < steps:
            relay(s)
        if s == steps - 1:
            for t in range(early, tiles):
                push(t)
        if 0 < s <= steps:
            hand_over(s - 1)
        if s < steps:
            serve_block(s, seat, False)
            serve_block(s, swap(seat), True)
        if s > 1:
            serve_block(s - 2, across, False)
            serve_block(s - 2, swap(across), True)

    for t in range(tiles):

        def wait_pot(k, _):
            source = fellow(k)
            pot_copy(t, source, source).wait_recv()
            return 0

        lax.fori_loop(1, near, wait_pot, 0)

        def advance(w, _):
            orbit = orb_ref[w].reshape(width, orb_ref.shape[-1])
            moved = jnp.dot(recv[t, w], orbit, preferred_element_type=jnp.float32)
            rows = pl.ds(home, near)
            old = orb_ref[w, rows, t].astype(jnp.float32)
            out_ref[w, rows, t] = (old + moved.reshape(old.shape)).astype(jnp.bfloat16)
            return 0

        lax.fori_loop(0, owned, advance, 0)

    def drain(k, _):
        peer = peer_of(k)
        remote(part.at[peer], part_in.at[peer], part_send.at[peer], part_recv.at[peer], peer).wait_send()
        remote(fields_own, fields_in.at[peer], field_send.at[peer], field_recv.at[peer], peer).wait_send()
        return 0

    lax.fori_loop(1, n, drain, 0)

    def drain_pot(k, _):
        for t in range(tiles):
            pot_copy(t, fellow(k), mine_at).wait_send()
        return 0

    lax.fori_loop(1, near, drain_pot, 0)
    for w in range(owned):
        host(w).wait_send()

        @pl.when(inner)
        def _():
            onward(w).wait_send()

    for s in range(steps):
        oz, w = block(s)
        slot = oz * PLANE + seat

        @pl.when(inner)
        def _():
            guest_copy(slot, w, relay_send.at[0, s], outward).wait_send()

        guest_copy(slot, w, relay_send.at[1, s], beside).wait_send()
        guest_copy(slot, w, relay_send.at[2, s], partner).wait_send()
        guest_copy(slot, w, pass_send.at[s], partner).wait_send()

    def collect(slot, _):
        for w in range(owned):
            done_copy(slot, w).wait_send()
            remote(
                done.at[slot, w], out_ref.at[w, away + slot], done_send.at[slot, w], done_recv.at[slot, w], away + slot
            ).wait_recv()
        return 0

    lax.fori_loop(0, near, collect, 0)


def on_device(n, chol_full, chol_half, green, gauss, orbitals):
    walkers, local_rows, nocc = green.shape
    owned, width, _ = orbitals.shape
    vectors = chol_half.shape[0]
    tiles = local_rows // TILE
    vmem = pl.BlockSpec(memory_space=pltpu.VMEM)
    hbm = pl.BlockSpec(memory_space=pl.ANY)
    dma = pltpu.SemaphoreType.DMA
    split = (owned, n, tiles, TILE, nocc)
    near = n // 2
    guests = near * orbitals.size * orbitals.dtype.itemsize
    relayed = n == 4 * PLANE and guests <= GUEST_LIMIT
    peers = near if relayed else n
    extra, extra_sems = [], []
    if relayed:
        planes = near // PLANE
        extra = [
            pltpu.VMEM((near,) + split, jnp.bfloat16),
            pltpu.VMEM((near, owned, tiles, TILE, nocc), jnp.bfloat16),
            pltpu.VMEM(split, jnp.bfloat16),
        ]
        extra_sems = [
            dma((owned,)), dma((near, owned)), dma((3, planes * owned)), dma((planes * owned,)),
            dma((near, owned)), dma((near, owned)), dma((owned,)), dma((owned,)),
        ]
    moved, logs = pl.pallas_call(
        functools.partial(relay_kernel if relayed else direct_kernel, n),
        out_shape=(
            jax.ShapeDtypeStruct(split, jnp.bfloat16),
            jax.ShapeDtypeStruct((owned, LANES), jnp.float32),
        ),
        in_specs=[hbm, hbm, hbm, vmem, vmem],
        out_specs=(vmem, vmem),
        scratch_shapes=[
            pltpu.VMEM((tiles, vectors, TILE, width), jnp.bfloat16),
            pltpu.VMEM((vectors, local_rows, nocc), jnp.bfloat16),
            pltpu.VMEM((walkers, local_rows, nocc), jnp.bfloat16),
            pltpu.VMEM((n, owned, vectors), jnp.float32),
            pltpu.VMEM((n, owned, vectors), jnp.float32),
            pltpu.VMEM((owned, vectors), jnp.float32),
            pltpu.VMEM((n, owned, vectors), jnp.float32),
            pltpu.VMEM((tiles, walkers, TILE, width), jnp.bfloat16),
            pltpu.VMEM((tiles, owned, peers * TILE, width), jnp.bfloat16),
            *extra,
            dma((tiles,)), dma((2,)), dma((n,)), dma((n,)), dma((n,)), dma((n,)),
            dma((tiles, peers)), dma((tiles, peers)), *extra_sems,
        ],
        compiler_params=pltpu.CompilerParams(
            collective_id=0, has_side_effects=True, vmem_limit_bytes=60 << 20
        ),
    )(chol_full, chol_half, green, gauss.reshape(n, owned, vectors), orbitals.reshape(split))
    return moved.reshape(orbitals.shape), logs[:, 0]


def solution(mesh):
    placed = (
        P(None, "chol", None),
        P(None, "chol", None),
        P("grp", "chol", None),
        P("grp", None),
        P(("grp", "chol"), None, None),
    )
    return jax.shard_map(
        functools.partial(on_device, mesh.shape["chol"]),
        mesh=mesh,
        in_specs=placed,
        out_specs=(P(("grp", "chol"), None, None), P(("grp", "chol"))),
        check_vma=False,
    )
```

profile of v0, /device:TPU:0, one launch (start us, length us, event | category | flops | bytes accessed | tf_op | source)
XLA Modules:
  0.0 204.0 jit_solution(602266556046832851)
XLA Ops:
  0.6 199.0 %shard_map.68 = (bf16[4,16,4,16,256]{4,3,2,1,0:T(8,128)(2,1)}, f32[4,128]{1,0:T(4,128)}) custom-call(bf16[128,64,1024]{2,1,0:T(8,128)(2,1)} %chol_hbm.1, bf16[128,64,256]{2,1,0:T(8,128)(2,1)} %half_hbm.1, bf16[64,64,256]{2,1,0:T(8,128)(2,1)} %green_hbm.1, f32[16,4,128]{2,1,0:T(4,128)} %bitcast.5, bf16[4,16,4,16,256]{4,3,2,1,0:T(8,128)(2,1)} %bitcast.3), custom_call_target="tpu_custom_call" | custom-call | tf_op jit(solution)/shard_map/pallas_call | solution.py:529
  199.7 1.3 slice_reduce_fusion
  201.0 3.0 %copy.8 = bf16[4,1024,256]{2,1,0:T(8,128)(2,1)} copy(bf16[4,1024,256]{2,1,0:T(8,128)(2,1)} %bitcast.4) | data formatting | bytes 4194304
where the time goes:
time: 204 us
  Pallas kernels  199 us (98%)
  local copies, waits for them, and re-layouts  4.36 us (2%)
    pallas_call x1, Pallas kernels, on_device(): pl.pallas_call(functools.partial(relay_kernel if relayed else direct_kern...  199 us

commit v1 on v0

--- a/solution.py
+++ b/solution.py
@@ -10,7 +10,10 @@
 TILE = 16
 LANES = 128
 PLANE = 4
-GUEST_LIMIT = 16 << 20
+OWN_LIMIT = 2 << 20
+CHUNKS = 2
+FIRST = 2
+SECOND = 3
 
 
 def remote(src, dst, send, recv, peer):
@@ -189,17 +192,33 @@
     lax.fori_loop(1, n, drain, 0)
 
 
-def relay_kernel(
+def line_kernel(
     n, chol_hbm, half_hbm, green_hbm, gauss_ref, orb_ref,
     out_ref, log_ref,
-    chol, half, green, part, part_in, fields_own, fields_in, send, recv, guest, done, hop,
+    chol, half, green, part, part_in, fields_own, fields_in, send, recv, guest, done, lent,
     load_sem, aux_sem, part_send, part_recv, field_send, field_recv, pot_send, pot_recv,
-    own_send, guest_recv, relay_send, pass_send, done_send, done_recv, hop_send, hop_recv,
+    orb_recv, ahead_send, back_send, lend_send, lend_recv, done_send, done_recv,
 ):
     me = lax.axis_index("chol")
     owned = part.shape[1]
     tiles = chol.shape[0]
     width = chol.shape[3]
+    nocc = orb_ref.shape[-1]
+    planes = n // PLANE
+    line = planes * owned
+    chunks = CHUNKS * owned
+    span = n // CHUNKS
+
+    z = me // PLANE
+    seat = lax.rem(me, PLANE)
+    side = z // 2
+    far = 1 - side
+    near_in, near_out = 1 + side, 3 * side
+    far_in, far_out = 1 + far, 3 * far
+    ahead = z + 1 - 2 * side
+    buddy = near_in + near_out - z
+    inner = z == near_in
+    outer = z == near_out
 
     half_copy = pltpu.make_async_copy(half_hbm, half, aux_sem.at[0])
     green_copy = pltpu.make_async_copy(green_hbm, green, aux_sem.at[1])
@@ -214,13 +233,47 @@
 
     barrier = pltpu.get_barrier_semaphore()
 
+    def peer_of(k):
+        return lax.rem(me + k, n)
+
     def greet(k, _):
         pl.semaphore_signal(
-            barrier, inc=1, device_id={"chol": lax.rem(me + k, n)}, device_id_type=pl.DeviceIdType.MESH
+            barrier, inc=1, device_id={"chol": peer_of(k)}, device_id_type=pl.DeviceIdType.MESH
         )
         return 0
 
     lax.fori_loop(1, n, greet, 0)
+    pl.semaphore_wait(barrier, n - 1)
+
+    def at(plane):
+        return plane * PLANE + seat
+
+    def piece(ref, c):
+        return ref.at[c // CHUNKS, pl.ds(lax.rem(c, CHUNKS) * span, span)]
+
+    def own_orbit(c):
+        return remote(piece(orb_ref, c), piece(guest.at[z], c), ahead_send.at[0, c], orb_recv.at[z, c], at(ahead))
+
+    def orbit_on(c):
+        there = piece(guest.at[near_out], c)
+        return remote(there, there, ahead_send.at[1, c], orb_recv.at[near_out, c], at(ahead))
+
+    def orbit_back(plane, k, c):
+        there = piece(guest.at[plane], c)
+        return remote(there, there, back_send.at[k, c], orb_recv.at[plane, c], at(buddy))
+
+    def await_orbit(plane, c):
+        there = piece(guest.at[plane], c)
+        remote(there, there, back_send.at[0, c], orb_recv.at[plane, c], at(ahead)).wait_recv()
+
+    def start_own(first, last):
+        def step(c, _):
+            own_orbit(c).start()
+            return 0
+
+        lax.fori_loop(first, last, step, 0)
+
+    start_own(0, FIRST)
 
     half_copy.wait()
     green_copy.wait()
@@ -238,10 +291,6 @@
     total = lax.fori_loop(0, tiles, bias, jnp.zeros((n * owned, half.shape[0]), jnp.float32))
     for d in range(n):
         part[d] = total[d * owned:(d + 1) * owned]
-    pl.semaphore_wait(barrier, n - 1)
-
-    def peer_of(k):
-        return lax.rem(me + k, n)
 
     def push_part(k, _):
         to = peer_of(k)
@@ -249,6 +298,7 @@
         return 0
 
     lax.fori_loop(1, n, push_part, 0)
+    start_own(FIRST, SECOND)
     part_in[me] = part[me]
 
     def wait_part(k, _):
@@ -274,6 +324,7 @@
         return 0
 
     lax.fori_loop(1, n, push_field, 0)
+    start_own(SECOND, chunks)
 
     def wait_field(k, _):
         peer = peer_of(k)
@@ -281,63 +332,35 @@
         return 0
 
     lax.fori_loop(1, n, wait_field, 0)
-    fields = jnp.concatenate([fields_in[d] for d in range(n)], axis=0).astype(jnp.bfloat16)
-
-    def walkers_of(d):
-        return pl.ds(d * owned, owned)
-
-    def rows_of(d):
-        return pl.ds(pl.multiple_of(d * TILE, TILE), TILE)
-
-    near = n // 2
-    planes = near // PLANE
-    mine_at = lax.rem(me, near)
-    home = me - mine_at
-    away = near - home
-    seat = lax.rem(me, PLANE)
-    across = lax.rem(seat + 2, PLANE)
-    upper = me // near
-    entry = away + (1 - upper) * 0 + upper * (near - PLANE) + seat
-    depth = upper * (mine_at // PLANE) + (1 - upper) * (planes - 1 - mine_at // PLANE)
-    outward = lax.rem(me + n + (2 * upper - 1) * PLANE, n)
-    inward = lax.rem(me + n - (2 * upper - 1) * PLANE, n)
-    partner = me + 1 - 2 * lax.rem(me, 2)
-    beside = me - seat + across
-
-    def swap(j):
-        return j + 1 - 2 * lax.rem(j, 2)
-
-    def guest_copy(slot, w, sem, to):
-        return remote(guest.at[slot, w], guest.at[slot, w], sem, guest_recv.at[slot, w], to)
-
-    inner = depth == 0
-    outer = depth > 0
-    behind = lax.rem(outward, near)
-
-    def host(w):
-        return remote(orb_ref.at[w], guest.at[mine_at, w], own_send.at[w], guest_recv.at[mine_at, w], entry)
-
-    def lift(w):
-        return remote(orb_ref.at[w], hop.at[w], own_send.at[w], hop_recv.at[w], inward)
-
-    def onward(w):
-        return remote(hop.at[w], guest.at[behind, w], hop_send.at[w], guest_recv.at[behind, w], entry)
-
-    @pl.when(inner)
-    def _():
-        for w in range(owned):
-            host(w).start()
-
-    @pl.when(outer)
-    def _():
-        for w in range(owned):
-            lift(w).start()
-
-    def forward(w):
-        @pl.when(inner)
-        def _():
-            lift(w).wait_recv()
-            onward(w).start()
+    fields = jnp.concatenate(
+        [fields_in[plane * PLANE + s] for s in range(PLANE) for plane in range(planes)], axis=0
+    ).astype(jnp.bfloat16)
+
+    groups = ((far * 2 * owned, 2 * owned), (buddy * owned, owned), (z * owned, owned))
+
+    def pot_copy(t, g, there, source):
+        first, count = groups[g]
+        return remote(
+            send.at[t, pl.ds(there * line + first, count)], recv.at[pl.ds(first, count), source, t],
+            pot_send.at[t, g, there], pot_recv.at[t, g, source], z * PLANE + there,
+        )
+
+    partner = seat + 1 - 2 * lax.rem(seat, 2)
+    beside = lax.rem(seat + 2, PLANE)
+    diagonal = lax.rem(partner + 2, PLANE)
+    others = (beside, diagonal, partner)
+
+    def push(t, g):
+        for s in others:
+            pot_copy(t, g, s, seat).start()
+
+    def await_pots(g, seats):
+        def step(t, _):
+            for s in seats:
+                pot_copy(t, g, s, s).wait_recv()
+            return 0
+
+        lax.fori_loop(0, tiles, step, 0)
 
     def fill(t):
         loads[t].wait()
@@ -353,109 +376,124 @@
             return 0
 
         lax.fori_loop(0, width // LANES, strip, 0)
-        recv[t, :, rows_of(mine_at), :] = send[t, walkers_of(me)]
-
-    def fellow(k):
-        return lax.rem(mine_at + k, near)
-
-    def pot_copy(t, there, source):
-        return remote(
-            send.at[t, walkers_of(home + there)], recv.at[t, :, rows_of(source), :],
-            pot_send.at[t, there], pot_recv.at[t, source], home + there,
-        )
-
-    def push(t):
-        def step(k, _):
-            pot_copy(t, fellow(k), mine_at).start()
-            return 0
-
-        lax.fori_loop(1, near, step, 0)
-
-    first = away // near
-
-    def block(s):
-        oz = s // owned
-        return (oz + (1 - 2 * oz) * (1 - first), s % owned)
-
-    def relay(s):
-        oz, w = block(s)
-        slot = oz * PLANE + seat
-        guest_copy(slot, w, own_send.at[w], partner).wait_recv()
-
+        recv[:, seat, t] = send[t, pl.ds(seat * line, line)]
+
+    def forward(first, last):
         @pl.when(inner)
         def _():
-            guest_copy(slot, w, relay_send.at[0, s], outward).start()
-
-        guest_copy(slot, w, relay_send.at[1, s], beside).start()
-        guest_copy(slot, w, relay_send.at[2, s], partner).start()
-
-    def hand_over(s):
-        oz, w = block(s)
-        slot = oz * PLANE + across
-        guest_copy(slot, w, own_send.at[w], partner).wait_recv()
-        guest_copy(slot, w, pass_send.at[s], partner).start()
-
-    def done_copy(slot, w):
-        return remote(
-            done.at[slot, w], out_ref.at[w, me], done_send.at[slot, w], done_recv.at[mine_at, w], away + slot
-        )
-
-    def serve(slot, w):
-        left = send[:, (away + slot) * owned + w].reshape(tiles * TILE, width)
-        orbit = guest[slot, w].reshape(width, guest.shape[-1])
-        moved = jnp.dot(left, orbit, preferred_element_type=jnp.float32)
-        old = guest[slot, w, me].astype(jnp.float32)
-        done[slot, w] = (old + moved.reshape(old.shape)).astype(jnp.bfloat16)
-        done_copy(slot, w).start()
-
-    def serve_block(s, j, wait):
-        oz, w = block(s)
-        slot = oz * PLANE + j
-        if wait:
-            guest_copy(slot, w, own_send.at[w], partner).wait_recv()
-        serve(slot, w)
-
-    steps = planes * owned
-    early = tiles - 1
+            def step(c, _):
+                await_orbit(near_out, c)
+                orbit_on(c).start()
+                await_orbit(far_in, c)
+                orbit_back(far_in, 0, c).start()
+                return 0
+
+            lax.fori_loop(first, last, step, 0)
+
+    def forward_far(first, last):
+        def step(c, _):
+            await_orbit(far_out, c)
+
+            @pl.when(inner)
+            def _():
+                orbit_back(far_out, 1, c).start()
+
+            return 0
+
+        lax.fori_loop(first, last, step, 0)
+
+    passed = 0
     for t in range(tiles):
         fill(t)
-        if t < early:
-            push(t)
-    for s in range(steps + 2):
-        if s < owned:
-            forward(s)
-        if s < steps:
-            relay(s)
-        if s == steps - 1:
-            for t in range(early, tiles):
-                push(t)
-        if 0 < s <= steps:
-            hand_over(s - 1)
-        if s < steps:
-            serve_block(s, seat, False)
-            serve_block(s, swap(seat), True)
-        if s > 1:
-            serve_block(s - 2, across, False)
-            serve_block(s - 2, swap(across), True)
-
-    for t in range(tiles):
-
-        def wait_pot(k, _):
-            source = fellow(k)
-            pot_copy(t, source, source).wait_recv()
-            return 0
-
-        lax.fori_loop(1, near, wait_pot, 0)
-
-        def advance(w, _):
-            orbit = orb_ref[w].reshape(width, orb_ref.shape[-1])
-            moved = jnp.dot(recv[t, w], orbit, preferred_element_type=jnp.float32)
-            rows = pl.ds(home, near)
-            old = orb_ref[w, rows, t].astype(jnp.float32)
-            out_ref[w, rows, t] = (old + moved.reshape(old.shape)).astype(jnp.bfloat16)
-            return 0
-
-        lax.fori_loop(0, owned, advance, 0)
+        push(t, 0)
+        last = chunks - (chunks >> (t + 1)) if t < tiles - 1 else chunks
+        forward(passed, last)
+        passed = last
+    for g in (1, 2):
+        for t in range(tiles):
+            push(t, g)
+
+    def lend(s):
+        return remote(
+            recv.at[pl.ds(buddy * owned, owned), s], lent.at[:, s], lend_send.at[s], lend_recv.at[s], at(buddy)
+        )
+
+    @pl.when(outer)
+    def _():
+        lend(seat).start()
+        await_pots(1, (partner,))
+        lend(partner).start()
+
+        def arrived(c, _):
+            await_orbit(far_in, c)
+            return 0
+
+        lax.fori_loop(0, chunks, arrived, 0)
+
+    def hand_back(plane, w):
+        return remote(
+            done.at[plane * owned + w], out_ref.at[w, pl.ds(z * PLANE, PLANE)],
+            done_send.at[plane, w], done_recv.at[z, w], at(plane),
+        )
+
+    def rows_done(left, orbit, old):
+        moved = jnp.dot(
+            left.reshape(-1, width), orbit.reshape(width, nocc), preferred_element_type=jnp.float32
+        )
+        return (old.astype(jnp.float32) + moved.reshape(old.shape)).astype(jnp.bfloat16)
+
+    here = pl.ds(z * PLANE, PLANE)
+
+    def serve(plane, first, last):
+        def step(w, _):
+            done[plane * owned + w] = rows_done(
+                recv[plane * owned + w], guest[plane, w], guest[plane, w, here]
+            )
+            hand_back(plane, w).start()
+            return 0
+
+        lax.fori_loop(first, last, step, 0)
+
+    ready = chunks * 5 // 8
+    forward_far(0, ready)
+    await_pots(0, others)
+    serve(far_in, 0, owned)
+    for w in range(owned):
+        if ready < CHUNKS * (w + 1):
+            forward_far(ready, CHUNKS * (w + 1))
+            ready = CHUNKS * (w + 1)
+        serve(far_out, w, w + 1)
+
+    @pl.when(outer)
+    def _():
+        for s in (beside, diagonal):
+            await_pots(1, (s,))
+            lend(s).start()
+
+    @pl.when(inner)
+    def _():
+        await_pots(1, others)
+        serve(near_out, 0, owned)
+
+    await_pots(2, others)
+
+    def advance(w, _):
+        out_ref[w, here] = rows_done(recv[z * owned + w], orb_ref[w], orb_ref[w, here])
+        return 0
+
+    lax.fori_loop(0, owned, advance, 0)
+
+    @pl.when(inner)
+    def _():
+        for s in (seat, partner, beside, diagonal):
+            lend(s).wait_recv()
+
+            def borrow(w, _):
+                row = near_out * PLANE + s
+                out_ref[w, row] = rows_done(lent[w, s], orb_ref[w], orb_ref[w, row])
+                return 0
+
+            lax.fori_loop(0, owned, borrow, 0)
 
     def drain(k, _):
         peer = peer_of(k)
@@ -465,40 +503,60 @@
 
     lax.fori_loop(1, n, drain, 0)
 
-    def drain_pot(k, _):
-        for t in range(tiles):
-            pot_copy(t, fellow(k), mine_at).wait_send()
-        return 0
-
-    lax.fori_loop(1, near, drain_pot, 0)
-    for w in range(owned):
-        host(w).wait_send()
+    def drain_pot(t, _):
+        for g in range(len(groups)):
+            for s in others:
+                pot_copy(t, g, s, seat).wait_send()
+        return 0
+
+    lax.fori_loop(0, tiles, drain_pot, 0)
+
+    def drain_orbit(c, _):
+        own_orbit(c).wait_send()
 
         @pl.when(inner)
         def _():
-            onward(w).wait_send()
-
-    for s in range(steps):
-        oz, w = block(s)
-        slot = oz * PLANE + seat
-
-        @pl.when(inner)
-        def _():
-            guest_copy(slot, w, relay_send.at[0, s], outward).wait_send()
-
-        guest_copy(slot, w, relay_send.at[1, s], beside).wait_send()
-        guest_copy(slot, w, relay_send.at[2, s], partner).wait_send()
-        guest_copy(slot, w, pass_send.at[s], partner).wait_send()
-
-    def collect(slot, _):
-        for w in range(owned):
-            done_copy(slot, w).wait_send()
+            orbit_on(c).wait_send()
+            orbit_back(far_in, 0, c).wait_send()
+            orbit_back(far_out, 1, c).wait_send()
+
+        return 0
+
+    lax.fori_loop(0, chunks, drain_orbit, 0)
+
+    @pl.when(outer)
+    def _():
+        for s in range(PLANE):
+            lend(s).wait_send()
+
+    def settle(plane):
+        def step(w, _):
             remote(
-                done.at[slot, w], out_ref.at[w, away + slot], done_send.at[slot, w], done_recv.at[slot, w], away + slot
+                done.at[plane * owned + w], out_ref.at[w, pl.ds(plane * PLANE, PLANE)],
+                done_send.at[plane, w], done_recv.at[plane, w], at(plane),
             ).wait_recv()
-        return 0
-
-    lax.fori_loop(0, near, collect, 0)
+            return 0
+
+        lax.fori_loop(0, owned, step, 0)
+
+    def flush(plane):
+        def step(w, _):
+            hand_back(plane, w).wait_send()
+            return 0
+
+        lax.fori_loop(0, owned, step, 0)
+
+    for plane in (far_in, far_out):
+        flush(plane)
+        settle(plane)
+
+    @pl.when(inner)
+    def _():
+        flush(near_out)
+
+    @pl.when(outer)
+    def _():
+        settle(near_in)
 
 
 def on_device(n, chol_full, chol_half, green, gauss, orbitals):
@@ -510,24 +568,27 @@
     hbm = pl.BlockSpec(memory_space=pl.ANY)
     dma = pltpu.SemaphoreType.DMA
     split = (owned, n, tiles, TILE, nocc)
-    near = n // 2
-    guests = near * orbitals.size * orbitals.dtype.itemsize
-    relayed = n == 4 * PLANE and guests <= GUEST_LIMIT
-    peers = near if relayed else n
-    extra, extra_sems = [], []
-    if relayed:
-        planes = near // PLANE
+    lined = n == 4 * PLANE and orbitals.size * orbitals.dtype.itemsize <= OWN_LIMIT
+    if lined:
+        line = walkers // PLANE
+        planes = n // PLANE
+        chunks = CHUNKS * owned
         extra = [
-            pltpu.VMEM((near,) + split, jnp.bfloat16),
-            pltpu.VMEM((near, owned, tiles, TILE, nocc), jnp.bfloat16),
-            pltpu.VMEM(split, jnp.bfloat16),
+            pltpu.VMEM((line, PLANE, tiles, TILE, width), jnp.bfloat16),
+            pltpu.VMEM((planes,) + split, jnp.bfloat16),
+            pltpu.VMEM((line, PLANE, tiles, TILE, nocc), jnp.bfloat16),
+            pltpu.VMEM((owned, PLANE, tiles, TILE, width), jnp.bfloat16),
         ]
         extra_sems = [
-            dma((owned,)), dma((near, owned)), dma((3, planes * owned)), dma((planes * owned,)),
-            dma((near, owned)), dma((near, owned)), dma((owned,)), dma((owned,)),
+            dma((tiles, 3, PLANE)), dma((tiles, 3, PLANE)),
+            dma((planes, chunks)), dma((2, chunks)), dma((2, chunks)),
+            dma((PLANE,)), dma((PLANE,)), dma((planes, owned)), dma((planes, owned)),
         ]
+    else:
+        extra = [pltpu.VMEM((tiles, owned, n * TILE, width), jnp.bfloat16)]
+        extra_sems = [dma((tiles, n)), dma((tiles, n))]
     moved, logs = pl.pallas_call(
-        functools.partial(relay_kernel if relayed else direct_kernel, n),
+        functools.partial(line_kernel if lined else direct_kernel, n),
         out_shape=(
             jax.ShapeDtypeStruct(split, jnp.bfloat16),
             jax.ShapeDtypeStruct((owned, LANES), jnp.float32),
@@ -543,10 +604,9 @@
             pltpu.VMEM((owned, vectors), jnp.float32),
             pltpu.VMEM((n, owned, vectors), jnp.float32),
             pltpu.VMEM((tiles, walkers, TILE, width), jnp.bfloat16),
-            pltpu.VMEM((tiles, owned, peers * TILE, width), jnp.bfloat16),
             *extra,
             dma((tiles,)), dma((2,)), dma((n,)), dma((n,)), dma((n,)), dma((n,)),
-            dma((tiles, peers)), dma((tiles, peers)), *extra_sems,
+            *extra_sems,
         ],
         compiler_params=pltpu.CompilerParams(
             collective_id=0, has_side_effects=True, vmem_limit_bytes=60 << 20

time: 204 us -> 179 us (0.88)
  the two profiles are of different devices: /device:TPU:0 before, /device:TPU:20 now
where the time goes in v1:
time: 179 us; the launch traced here: 178 us
  Pallas kernels  173 us (97%)
  local copies, waits for them, and re-layouts  4.36 us (2%)
    pallas_call x1, Pallas kernels, on_device(): pl.pallas_call(functools.partial(line_kernel if lined else direct_kernel,...  173 us

profile of v1, /device:TPU:20, one launch (start us, length us, event | category | flops | bytes accessed | tf_op | source)
XLA Modules:
  0.0 178.4 jit_solution(42534403546620423)
XLA Ops:
  0.6 173.4 %shard_map.68 = (bf16[4,16,4,16,256]{4,3,2,1,0:T(8,128)(2,1)}, f32[4,128]{1,0:T(4,128)}) custom-call(bf16[128,64,1024]{2,1,0:T(8,128)(2,1)} %chol_hbm.1, bf16[128,64,256]{2,1,0:T(8,128)(2,1)} %half_hbm.1, bf16[64,64,256]{2,1,0:T(8,128)(2,1)} %green_hbm.1, f32[16,4,128]{2,1,0:T(4,128)} %bitcast.5, bf16[4,16,4,16,256]{4,3,2,1,0:T(8,128)(2,1)} %bitcast.3), custom_call_target="tpu_custom_call" | custom-call | tf_op jit(solution)/shard_map/pallas_call | solution.py:590
  174.1 1.3 slice_reduce_fusion
  175.4 3.0 %copy.8 = bf16[4,1024,256]{2,1,0:T(8,128)(2,1)} copy(bf16[4,1024,256]{2,1,0:T(8,128)(2,1)} %bitcast.4) | data formatting | bytes 4194304

commit v2 on v1

--- a/solution.py
+++ b/solution.py
@@ -273,6 +273,26 @@
 
         lax.fori_loop(first, last, step, 0)
 
+    def pass_on(first, last):
+        @pl.when(inner)
+        def _():
+            def step(c, _):
+                await_orbit(near_out, c)
+                orbit_on(c).start()
+                return 0
+
+            lax.fori_loop(first, last, step, 0)
+
+    def pass_back(first, last):
+        @pl.when(inner)
+        def _():
+            def step(c, _):
+                await_orbit(far_in, c)
+                orbit_back(far_in, 0, c).start()
+                return 0
+
+            lax.fori_loop(first, last, step, 0)
+
     start_own(0, FIRST)
 
     half_copy.wait()
@@ -299,6 +319,7 @@
 
     lax.fori_loop(1, n, push_part, 0)
     start_own(FIRST, SECOND)
+    pass_back(0, FIRST)
     part_in[me] = part[me]
 
     def wait_part(k, _):
@@ -325,6 +346,7 @@
 
     lax.fori_loop(1, n, push_field, 0)
     start_own(SECOND, chunks)
+    pass_back(FIRST, SECOND)
 
     def wait_field(k, _):
         peer = peer_of(k)
@@ -378,18 +400,6 @@
         lax.fori_loop(0, width // LANES, strip, 0)
         recv[:, seat, t] = send[t, pl.ds(seat * line, line)]
 
-    def forward(first, last):
-        @pl.when(inner)
-        def _():
-            def step(c, _):
-                await_orbit(near_out, c)
-                orbit_on(c).start()
-                await_orbit(far_in, c)
-                orbit_back(far_in, 0, c).start()
-                return 0
-
-            lax.fori_loop(first, last, step, 0)
-
     def forward_far(first, last):
         def step(c, _):
             await_orbit(far_out, c)
@@ -402,13 +412,12 @@
 
         lax.fori_loop(first, last, step, 0)
 
-    passed = 0
     for t in range(tiles):
         fill(t)
         push(t, 0)
-        last = chunks - (chunks >> (t + 1)) if t < tiles - 1 else chunks
-        forward(passed, last)
-        passed = last
+        if t < tiles - 2:
+            pass_back(SECOND + t, SECOND + t + 1)
+    held = SECOND + tiles - 2
     for g in (1, 2):
         for t in range(tiles):
             push(t, g)
@@ -418,6 +427,11 @@
             recv.at[pl.ds(buddy * owned, owned), s], lent.at[:, s], lend_send.at[s], lend_recv.at[s], at(buddy)
         )
 
+    pass_on(0, held + 1)
+    pass_back(held, held + 2)
+    pass_on(held + 1, held + 2)
+    pass_back(held + 2, chunks)
+    pass_on(held + 2, chunks)
     @pl.when(outer)
     def _():
         lend(seat).start()
@@ -463,12 +477,12 @@
             forward_far(ready, CHUNKS * (w + 1))
             ready = CHUNKS * (w + 1)
         serve(far_out, w, w + 1)
-
-    @pl.when(outer)
-    def _():
-        for s in (beside, diagonal):
-            await_pots(1, (s,))
-            lend(s).start()
+        if w == owned - 2:
+            @pl.when(outer)
+            def _():
+                for s in (beside, diagonal):
+                    await_pots(1, (s,))
+                    lend(s).start()
 
     @pl.when(inner)
     def _():

time: 179 us -> 161 us (0.90)
  the two profiles are of different devices: /device:TPU:20 before, /device:TPU:0 now
where the time goes in v2:
time: 161 us
  Pallas kernels  156 us (97%)
  local copies, waits for them, and re-layouts  4.36 us (3%)
    pallas_call x1, Pallas kernels, on_device(): pl.pallas_call(functools.partial(line_kernel if lined else direct_kernel,...  156 us

profile of v2, /device:TPU:0, one launch (start us, length us, event | category | flops | bytes accessed | tf_op | source)
XLA Modules:
  0.0 160.8 jit_solution(7499957925063638445)
XLA Ops:
  0.6 155.8 %shard_map.68 = (bf16[4,16,4,16,256]{4,3,2,1,0:T(8,128)(2,1)}, f32[4,128]{1,0:T(4,128)}) custom-call(bf16[128,64,1024]{2,1,0:T(8,128)(2,1)} %chol_hbm.1, bf16[128,64,256]{2,1,0:T(8,128)(2,1)} %half_hbm.1, bf16[64,64,256]{2,1,0:T(8,128)(2,1)} %green_hbm.1, f32[16,4,128]{2,1,0:T(4,128)} %bitcast.5, bf16[4,16,4,16,256]{4,3,2,1,0:T(8,128)(2,1)} %bitcast.3), custom_call_target="tpu_custom_call" | custom-call | tf_op jit(solution)/shard_map/pallas_call | solution.py:604
  156.4 1.3 slice_reduce_fusion
  157.7 3.0 %copy.8 = bf16[4,1024,256]{2,1,0:T(8,128)(2,1)} copy(bf16[4,1024,256]{2,1,0:T(8,128)(2,1)} %bitcast.4) | data formatting | bytes 4194304

commit v3 on v2

--- a/solution.py
+++ b/solution.py
@@ -358,13 +358,16 @@
         [fields_in[plane * PLANE + s] for s in range(PLANE) for plane in range(planes)], axis=0
     ).astype(jnp.bfloat16)
 
-    groups = ((far * 2 * owned, 2 * owned), (buddy * owned, owned), (z * owned, owned))
-
-    def pot_copy(t, g, there, source):
-        first, count = groups[g]
+    order = (
+        jnp.where(inner, far_in, near_in), jnp.where(inner, far_out, far_in),
+        jnp.where(inner, near_out, far_out), z,
+    )
+
+    def pot_copy(t, plane, there, source):
         return remote(
-            send.at[t, pl.ds(there * line + first, count)], recv.at[pl.ds(first, count), source, t],
-            pot_send.at[t, g, there], pot_recv.at[t, g, source], z * PLANE + there,
+            send.at[t, pl.ds(there * line + plane * owned, owned)],
+            recv.at[pl.ds(plane * owned, owned), source, t],
+            pot_send.at[t, plane, there], pot_recv.at[t, plane, source], z * PLANE + there,
         )
 
     partner = seat + 1 - 2 * lax.rem(seat, 2)
@@ -372,14 +375,14 @@
     diagonal = lax.rem(partner + 2, PLANE)
     others = (beside, diagonal, partner)
 
-    def push(t, g):
+    def push(t, plane):
         for s in others:
-            pot_copy(t, g, s, seat).start()
-
-    def await_pots(g, seats):
+            pot_copy(t, plane, s, seat).start()
+
+    def await_pots(plane, seats):
         def step(t, _):
             for s in seats:
-                pot_copy(t, g, s, s).wait_recv()
+                pot_copy(t, plane, s, s).wait_recv()
             return 0
 
         lax.fori_loop(0, tiles, step, 0)
@@ -414,13 +417,13 @@
 
     for t in range(tiles):
         fill(t)
-        push(t, 0)
+        push(t, order[0])
         if t < tiles - 2:
             pass_back(SECOND + t, SECOND + t + 1)
     held = SECOND + tiles - 2
-    for g in (1, 2):
+    for plane in order[1:]:
         for t in range(tiles):
-            push(t, g)
+            push(t, plane)
 
     def lend(s):
         return remote(
@@ -435,8 +438,9 @@
     @pl.when(outer)
     def _():
         lend(seat).start()
-        await_pots(1, (partner,))
-        lend(partner).start()
+        for s in (partner, beside, diagonal):
+            await_pots(near_in, (s,))
+            lend(s).start()
 
         def arrived(c, _):
             await_orbit(far_in, c)
@@ -468,28 +472,22 @@
 
         lax.fori_loop(first, last, step, 0)
 
-    ready = chunks * 5 // 8
-    forward_far(0, ready)
-    await_pots(0, others)
+    forward_far(0, CHUNKS)
+    await_pots(far_in, others)
     serve(far_in, 0, owned)
-    for w in range(owned):
-        if ready < CHUNKS * (w + 1):
-            forward_far(ready, CHUNKS * (w + 1))
-            ready = CHUNKS * (w + 1)
+    forward_far(CHUNKS, 2 * CHUNKS)
+    await_pots(far_out, others)
+    serve(far_out, 0, 2)
+    for w in range(2, owned):
+        forward_far(CHUNKS * w, CHUNKS * (w + 1))
         serve(far_out, w, w + 1)
-        if w == owned - 2:
-            @pl.when(outer)
-            def _():
-                for s in (beside, diagonal):
-                    await_pots(1, (s,))
-                    lend(s).start()
 
     @pl.when(inner)
     def _():
-        await_pots(1, others)
+        await_pots(near_out, others)
         serve(near_out, 0, owned)
 
-    await_pots(2, others)
+    await_pots(z, others)
 
     def advance(w, _):
         out_ref[w, here] = rows_done(recv[z * owned + w], orb_ref[w], orb_ref[w, here])
@@ -518,9 +516,9 @@
     lax.fori_loop(1, n, drain, 0)
 
     def drain_pot(t, _):
-        for g in range(len(groups)):
+        for plane in range(planes):
             for s in others:
-                pot_copy(t, g, s, seat).wait_send()
+                pot_copy(t, plane, s, seat).wait_send()
         return 0
 
     lax.fori_loop(0, tiles, drain_pot, 0)
@@ -594,7 +592,7 @@
             pltpu.VMEM((owned, PLANE, tiles, TILE, width), jnp.bfloat16),
         ]
         extra_sems = [
-            dma((tiles, 3, PLANE)), dma((tiles, 3, PLANE)),
+            dma((tiles, planes, PLANE)), dma((tiles, planes, PLANE)),
             dma((planes, chunks)), dma((2, chunks)), dma((2, chunks)),
             dma((PLANE,)), dma((PLANE,)), dma((planes, owned)), dma((planes, owned)),
         ]

time: 161 us -> 155 us (0.963)
  Pallas kernels: 156 us -> 150 us
    pallas_call x1, Pallas kernels: 156 us -> 150 us  [on_device(): pl.pallas_call(functools.partial(line_kernel if lined else direct_kernel,...]
where the time goes in v3:
time: 155 us
  Pallas kernels  150 us (97%)
  local copies, waits for them, and re-layouts  4.36 us (3%)
    pallas_call x1, Pallas kernels, on_device(): pl.pallas_call(functools.partial(line_kernel if lined else direct_kernel,...  150 us

profile of v3, /device:TPU:0, one launch (start us, length us, event | category | flops | bytes accessed | tf_op | source)
XLA Modules:
  0.0 154.5 jit_solution(463278407996482562)
XLA Ops:
  0.6 149.5 %shard_map.68 = (bf16[4,16,4,16,256]{4,3,2,1,0:T(8,128)(2,1)}, f32[4,128]{1,0:T(4,128)}) custom-call(bf16[128,64,1024]{2,1,0:T(8,128)(2,1)} %chol_hbm.1, bf16[128,64,256]{2,1,0:T(8,128)(2,1)} %half_hbm.1, bf16[64,64,256]{2,1,0:T(8,128)(2,1)} %green_hbm.1, f32[16,4,128]{2,1,0:T(4,128)} %bitcast.5, bf16[4,16,4,16,256]{4,3,2,1,0:T(8,128)(2,1)} %bitcast.3), custom_call_target="tpu_custom_call" | custom-call | tf_op jit(solution)/shard_map/pallas_call | solution.py:602
  150.2 1.3 slice_reduce_fusion
  151.5 3.0 %copy.8 = bf16[4,1024,256]{2,1,0:T(8,128)(2,1)} copy(bf16[4,1024,256]{2,1,0:T(8,128)(2,1)} %bitcast.4) | data formatting | bytes 4194304

commit v4 on v3

--- a/solution.py
+++ b/solution.py
@@ -12,8 +12,8 @@
 PLANE = 4
 OWN_LIMIT = 2 << 20
 CHUNKS = 2
-FIRST = 2
-SECOND = 3
+FIRST = 1
+SECOND = 2
 
 
 def remote(src, dst, send, recv, peer):
@@ -193,11 +193,11 @@
 
 
 def line_kernel(
-    n, chol_hbm, half_hbm, green_hbm, gauss_ref, orb_ref,
+    n, chol_hbm, half_hbm, green_hbm, gauss_hbm, orb_hbm,
     out_ref, log_ref,
-    chol, half, green, part, part_in, fields_own, fields_in, send, recv, guest, done, lent,
-    load_sem, aux_sem, part_send, part_recv, field_send, field_recv, pot_send, pot_recv,
-    orb_recv, ahead_send, back_send, lend_send, lend_recv, done_send, done_recv,
+    chol, half, green, gauss_ref, orb_ref, part, part_in, fields_own, fields_in, send, recv, guest, done, lent,
+    load_sem, aux_sem, part_sem, field_sem, pot_send, pot_recv, orb_send, orb_recv,
+    lend_send, lend_recv, done_send, done_recv,
 ):
     me = lax.axis_index("chol")
     owned = part.shape[1]
@@ -222,15 +222,14 @@
 
     half_copy = pltpu.make_async_copy(half_hbm, half, aux_sem.at[0])
     green_copy = pltpu.make_async_copy(green_hbm, green, aux_sem.at[1])
-    half_copy.start()
-    green_copy.start()
+    gauss_copy = pltpu.make_async_copy(gauss_hbm, gauss_ref, aux_sem.at[2])
+    orb_copy = pltpu.make_async_copy(orb_hbm, orb_ref, aux_sem.at[3])
+    for copy in (orb_copy, green_copy, half_copy, gauss_copy):
+        copy.start()
     loads = [
         pltpu.make_async_copy(chol_hbm.at[:, pl.ds(t * TILE, TILE), :], chol.at[t], load_sem.at[t])
         for t in range(tiles)
     ]
-    for load in loads:
-        load.start()
-
     barrier = pltpu.get_barrier_semaphore()
 
     def peer_of(k):
@@ -252,19 +251,19 @@
         return ref.at[c // CHUNKS, pl.ds(lax.rem(c, CHUNKS) * span, span)]
 
     def own_orbit(c):
-        return remote(piece(orb_ref, c), piece(guest.at[z], c), ahead_send.at[0, c], orb_recv.at[z, c], at(ahead))
+        return remote(piece(orb_ref, c), piece(guest.at[z], c), orb_send.at[0], orb_recv.at[z, c], at(ahead))
 
     def orbit_on(c):
         there = piece(guest.at[near_out], c)
-        return remote(there, there, ahead_send.at[1, c], orb_recv.at[near_out, c], at(ahead))
+        return remote(there, there, orb_send.at[1], orb_recv.at[near_out, c], at(ahead))
 
     def orbit_back(plane, k, c):
         there = piece(guest.at[plane], c)
-        return remote(there, there, back_send.at[k, c], orb_recv.at[plane, c], at(buddy))
+        return remote(there, there, orb_send.at[k], orb_recv.at[plane, c], at(buddy))
 
     def await_orbit(plane, c):
         there = piece(guest.at[plane], c)
-        remote(there, there, back_send.at[0, c], orb_recv.at[plane, c], at(ahead)).wait_recv()
+        remote(there, there, orb_send.at[0], orb_recv.at[plane, c], at(ahead)).wait_recv()
 
     def start_own(first, last):
         def step(c, _):
@@ -288,15 +287,19 @@
         def _():
             def step(c, _):
                 await_orbit(far_in, c)
-                orbit_back(far_in, 0, c).start()
+                orbit_back(far_in, 2, c).start()
                 return 0
 
             lax.fori_loop(first, last, step, 0)
 
+    orb_copy.wait()
     start_own(0, FIRST)
 
     half_copy.wait()
     green_copy.wait()
+    for load in loads:
+        load.start()
+    gauss_copy.wait()
 
     def bias(t, acc):
         rows = pl.ds(pl.multiple_of(t * TILE, TILE), TILE)
@@ -314,7 +317,7 @@
 
     def push_part(k, _):
         to = peer_of(k)
-        remote(part.at[to], part_in.at[me], part_send.at[to], part_recv.at[me], to).start()
+        remote(part.at[to], part_in.at[me], part_sem.at[0], part_sem.at[1], to).start()
         return 0
 
     lax.fori_loop(1, n, push_part, 0)
@@ -322,13 +325,11 @@
     pass_back(0, FIRST)
     part_in[me] = part[me]
 
-    def wait_part(k, _):
-        peer = peer_of(k)
-        copy = remote(part.at[peer], part_in.at[peer], part_send.at[peer], part_recv.at[peer], peer)
-        copy.wait_recv()
-        return 0
-
-    lax.fori_loop(1, n, wait_part, 0)
+    def gathered(ref, sem):
+        every = ref.at[pl.ds(0, n - 1)]
+        return remote(every, every, sem.at[0], sem.at[1], peer_of(1))
+
+    gathered(part_in, part_sem).wait_recv()
     vbias = jnp.sum(part_in[...], axis=0)
     gauss = gauss_ref[me]
     xbar = jnp.clip(-0.3 * vbias, -1.0, 1.0)
@@ -341,19 +342,14 @@
 
     def push_field(k, _):
         to = peer_of(k)
-        remote(fields_own, fields_in.at[me], field_send.at[to], field_recv.at[me], to).start()
+        remote(fields_own, fields_in.at[me], field_sem.at[0], field_sem.at[1], to).start()
         return 0
 
     lax.fori_loop(1, n, push_field, 0)
     start_own(SECOND, chunks)
     pass_back(FIRST, SECOND)
 
-    def wait_field(k, _):
-        peer = peer_of(k)
-        remote(fields_own, fields_in.at[peer], field_send.at[peer], field_recv.at[peer], peer).wait_recv()
-        return 0
-
-    lax.fori_loop(1, n, wait_field, 0)
+    gathered(fields_in, field_sem).wait_recv()
     fields = jnp.concatenate(
         [fields_in[plane * PLANE + s] for s in range(PLANE) for plane in range(planes)], axis=0
     ).astype(jnp.bfloat16)
@@ -367,7 +363,7 @@
         return remote(
             send.at[t, pl.ds(there * line + plane * owned, owned)],
             recv.at[pl.ds(plane * owned, owned), source, t],
-            pot_send.at[t, plane, there], pot_recv.at[t, plane, source], z * PLANE + there,
+            pot_send.at[0], pot_recv.at[plane, source], z * PLANE + there,
         )
 
     partner = seat + 1 - 2 * lax.rem(seat, 2)
@@ -380,12 +376,9 @@
             pot_copy(t, plane, s, seat).start()
 
     def await_pots(plane, seats):
-        def step(t, _):
-            for s in seats:
-                pot_copy(t, plane, s, s).wait_recv()
-            return 0
-
-        lax.fori_loop(0, tiles, step, 0)
+        for s in seats:
+            every = recv.at[pl.ds(plane * owned, owned), s]
+            remote(every, every, pot_send.at[0], pot_recv.at[plane, s], z * PLANE + partner).wait_recv()
 
     def fill(t):
         loads[t].wait()
@@ -409,7 +402,7 @@
 
             @pl.when(inner)
             def _():
-                orbit_back(far_out, 1, c).start()
+                orbit_back(far_out, 3, c).start()
 
             return 0
 
@@ -427,7 +420,7 @@
 
     def lend(s):
         return remote(
-            recv.at[pl.ds(buddy * owned, owned), s], lent.at[:, s], lend_send.at[s], lend_recv.at[s], at(buddy)
+            recv.at[pl.ds(buddy * owned, owned), s], lent.at[:, s], lend_send.at[0], lend_recv.at[s], at(buddy)
         )
 
     pass_on(0, held + 1)
@@ -451,7 +444,7 @@
     def hand_back(plane, w):
         return remote(
             done.at[plane * owned + w], out_ref.at[w, pl.ds(z * PLANE, PLANE)],
-            done_send.at[plane, w], done_recv.at[z, w], at(plane),
+            done_send.at[plane], done_recv.at[z], at(plane),
         )
 
     def rows_done(left, orbit, old):
@@ -507,64 +500,33 @@
 
             lax.fori_loop(0, owned, borrow, 0)
 
-    def drain(k, _):
-        peer = peer_of(k)
-        remote(part.at[peer], part_in.at[peer], part_send.at[peer], part_recv.at[peer], peer).wait_send()
-        remote(fields_own, fields_in.at[peer], field_send.at[peer], field_recv.at[peer], peer).wait_send()
-        return 0
-
-    lax.fori_loop(1, n, drain, 0)
-
-    def drain_pot(t, _):
-        for plane in range(planes):
-            for s in others:
-                pot_copy(t, plane, s, seat).wait_send()
-        return 0
-
-    lax.fori_loop(0, tiles, drain_pot, 0)
-
-    def drain_orbit(c, _):
-        own_orbit(c).wait_send()
-
-        @pl.when(inner)
-        def _():
-            orbit_on(c).wait_send()
-            orbit_back(far_in, 0, c).wait_send()
-            orbit_back(far_out, 1, c).wait_send()
-
-        return 0
-
-    lax.fori_loop(0, chunks, drain_orbit, 0)
+    gathered(part_in, part_sem).wait_send()
+    gathered(fields_in, field_sem).wait_send()
+    every = send.at[:, pl.ds(0, (PLANE - 1) * line)]
+    remote(every, every, pot_send.at[0], pot_recv.at[z, seat], at(ahead)).wait_send()
+
+    def sent(ref, sem):
+        remote(ref, ref, sem, lend_recv.at[0], at(ahead)).wait_send()
+
+    sent(orb_ref, orb_send.at[0])
+
+    @pl.when(inner)
+    def _():
+        for k in range(1, 4):
+            sent(guest.at[0], orb_send.at[k])
+        sent(done.at[pl.ds(0, owned)], done_send.at[near_out])
 
     @pl.when(outer)
     def _():
-        for s in range(PLANE):
-            lend(s).wait_send()
+        sent(lent, lend_send.at[0])
 
     def settle(plane):
-        def step(w, _):
-            remote(
-                done.at[plane * owned + w], out_ref.at[w, pl.ds(plane * PLANE, PLANE)],
-                done_send.at[plane, w], done_recv.at[plane, w], at(plane),
-            ).wait_recv()
-            return 0
-
-        lax.fori_loop(0, owned, step, 0)
-
-    def flush(plane):
-        def step(w, _):
-            hand_back(plane, w).wait_send()
-            return 0
-
-        lax.fori_loop(0, owned, step, 0)
+        block = out_ref.at[:, pl.ds(plane * PLANE, PLANE)]
+        remote(block, block, done_send.at[plane], done_recv.at[plane], at(plane)).wait_recv()
 
     for plane in (far_in, far_out):
-        flush(plane)
+        sent(done.at[pl.ds(0, owned)], done_send.at[plane])
         settle(plane)
-
-    @pl.when(inner)
-    def _():
-        flush(near_out)
 
     @pl.when(outer)
     def _():
@@ -580,50 +542,60 @@
     hbm = pl.BlockSpec(memory_space=pl.ANY)
     dma = pltpu.SemaphoreType.DMA
     split = (owned, n, tiles, TILE, nocc)
-    lined = n == 4 * PLANE and orbitals.size * orbitals.dtype.itemsize <= OWN_LIMIT
-    if lined:
+    params = pltpu.CompilerParams(collective_id=0, has_side_effects=True, vmem_limit_bytes=60 << 20)
+    shared = [
+        pltpu.VMEM((tiles, vectors, TILE, width), jnp.bfloat16),
+        pltpu.VMEM((vectors, local_rows, nocc), jnp.bfloat16),
+        pltpu.VMEM((walkers, local_rows, nocc), jnp.bfloat16),
+    ]
+    sums = [
+        pltpu.VMEM((n, owned, vectors), jnp.float32),
+        pltpu.VMEM((n, owned, vectors), jnp.float32),
+        pltpu.VMEM((owned, vectors), jnp.float32),
+        pltpu.VMEM((n, owned, vectors), jnp.float32),
+        pltpu.VMEM((tiles, walkers, TILE, width), jnp.bfloat16),
+    ]
+    arrays = (chol_full, chol_half, green, gauss.reshape(n, owned, vectors), orbitals.reshape(split))
+    if n == 4 * PLANE and orbitals.size * orbitals.dtype.itemsize <= OWN_LIMIT:
         line = walkers // PLANE
         planes = n // PLANE
-        chunks = CHUNKS * owned
-        extra = [
-            pltpu.VMEM((line, PLANE, tiles, TILE, width), jnp.bfloat16),
-            pltpu.VMEM((planes,) + split, jnp.bfloat16),
-            pltpu.VMEM((line, PLANE, tiles, TILE, nocc), jnp.bfloat16),
-            pltpu.VMEM((owned, PLANE, tiles, TILE, width), jnp.bfloat16),
-        ]
-        extra_sems = [
-            dma((tiles, planes, PLANE)), dma((tiles, planes, PLANE)),
-            dma((planes, chunks)), dma((2, chunks)), dma((2, chunks)),
-            dma((PLANE,)), dma((PLANE,)), dma((planes, owned)), dma((planes, owned)),
-        ]
+        moved, logs = pl.pallas_call(
+            functools.partial(line_kernel, n),
+            out_shape=(pltpu.VMEM(split, jnp.bfloat16), pltpu.VMEM((owned, LANES), jnp.float32)),
+            in_specs=[hbm] * 5,
+            out_specs=(vmem, vmem),
+            scratch_shapes=[
+                *shared,
+                pltpu.VMEM((n, owned, vectors), jnp.float32),
+                pltpu.VMEM(split, jnp.bfloat16),
+                *sums,
+                pltpu.VMEM((line, PLANE, tiles, TILE, width), jnp.bfloat16),
+                pltpu.VMEM((planes,) + split, jnp.bfloat16),
+                pltpu.VMEM((line, PLANE, tiles, TILE, nocc), jnp.bfloat16),
+                pltpu.VMEM((owned, PLANE, tiles, TILE, width), jnp.bfloat16),
+                dma((tiles,)), dma((4,)), dma((2,)), dma((2,)), dma((1,)), dma((planes, PLANE)),
+                dma((4,)), dma((planes, CHUNKS * owned)), dma((1,)), dma((PLANE,)), dma((planes,)), dma((planes,)),
+            ],
+            compiler_params=params,
+        )(*arrays)
     else:
-        extra = [pltpu.VMEM((tiles, owned, n * TILE, width), jnp.bfloat16)]
-        extra_sems = [dma((tiles, n)), dma((tiles, n))]
-    moved, logs = pl.pallas_call(
-        functools.partial(line_kernel if lined else direct_kernel, n),
-        out_shape=(
-            jax.ShapeDtypeStruct(split, jnp.bfloat16),
-            jax.ShapeDtypeStruct((owned, LANES), jnp.float32),
-        ),
-        in_specs=[hbm, hbm, hbm, vmem, vmem],
-        out_specs=(vmem, vmem),
-        scratch_shapes=[
-            pltpu.VMEM((tiles, vectors, TILE, width), jnp.bfloat16),
-            pltpu.VMEM((vectors, local_rows, nocc), jnp.bfloat16),
-            pltpu.VMEM((walkers, local_rows, nocc), jnp.bfloat16),
-            pltpu.VMEM((n, owned, vectors), jnp.float32),
-            pltpu.VMEM((n, owned, vectors), jnp.float32),
-            pltpu.VMEM((owned, vectors), jnp.float32),
-            pltpu.VMEM((n, owned, vectors), jnp.float32),
-            pltpu.VMEM((tiles, walkers, TILE, width), jnp.bfloat16),
-            *extra,
-            dma((tiles,)), dma((2,)), dma((n,)), dma((n,)), dma((n,)), dma((n,)),
-            *extra_sems,
-        ],
-        compiler_params=pltpu.CompilerParams(
-            collective_id=0, has_side_effects=True, vmem_limit_bytes=60 << 20
-        ),
-    )(chol_full, chol_half, green, gauss.reshape(n, owned, vectors), orbitals.reshape(split))
+        moved, logs = pl.pallas_call(
+            functools.partial(direct_kernel, n),
+            out_shape=(
+                jax.ShapeDtypeStruct(split, jnp.bfloat16),
+                jax.ShapeDtypeStruct((owned, LANES), jnp.float32),
+            ),
+            in_specs=[hbm, hbm, hbm, vmem, vmem],
+            out_specs=(vmem, vmem),
+            scratch_shapes=[
+                *shared,
+                *sums,
+                pltpu.VMEM((tiles, owned, n * TILE, width), jnp.bfloat16),
+                dma((tiles,)), dma((2,)), dma((n,)), dma((n,)), dma((n,)), dma((n,)),
+                dma((tiles, n)), dma((tiles, n)),
+            ],
+            compiler_params=params,
+        )(*arrays)
     return moved.reshape(orbitals.shape), logs[:, 0]
 
 

time: 155 us -> 147 us (0.948)
  Pallas kernels: 150 us -> 145 us
  local copies, waits for them, and re-layouts: 4.36 us -> 1.95 us
    pallas_call x1, Pallas kernels: 150 us -> 145 us  [on_device(): pl.pallas_call(functools.partial(line_kernel, n), out_shape=(pltpu.VMEM(s...]
    unnamed x1, local copies, waits for them, and re-layouts: 3.04 us -> 1.32 us
where the time goes in v4:
time: 147 us
  Pallas kernels  145 us (99%)
  local copies, waits for them, and re-layouts  1.95 us (1%)
    pallas_call x1, Pallas kernels, on_device(): pl.pallas_call(functools.partial(line_kernel, n), out_shape=(pltpu.VMEM(s...  145 us

profile of v4, /device:TPU:0, one launch (start us, length us, event | category | flops | bytes accessed | tf_op | source)
XLA Modules:
  0.0 147.3 jit_solution(12321983168302876653)
XLA Ops:
  0.6 144.7 %shard_map.68 = (bf16[4,16,4,16,256]{4,3,2,1,0:T(8,128)(2,1)S(1)}, f32[4,128]{1,0:T(4,128)S(1)}) custom-call(bf16[128,64,1024]{2,1,0:T(8,128)(2,1)} %chol_hbm.1, bf16[128,64,256]{2,1,0:T(8,128)(2,1)} %half_hbm.1, bf16[64,64,256]{2,1,0:T(8,128)(2,1)} %green_hbm.1, f32[16,4,128]{2,1,0:T(4,128)} %bitcast.5, bf16[4,16,4,16,256]{4,3,2,1,0:T(8,128)(2,1)} %bitcast.4), custom_call_target="tpu_custom_call" | custom-call | tf_op jit(solution)/shard_map/pallas_call | solution.py:562
  145.4 1.3 copy.8
  146.7 0.6 slice_reduce_fusion

commit v5 on v4

--- a/solution.py
+++ b/solution.py
@@ -14,6 +14,7 @@
 CHUNKS = 2
 FIRST = 1
 SECOND = 2
+THIRD = 3
 
 
 def remote(src, dst, send, recv, peer):
@@ -195,12 +196,13 @@
 def line_kernel(
     n, chol_hbm, half_hbm, green_hbm, gauss_hbm, orb_hbm,
     out_ref, log_ref,
-    chol, half, green, gauss_ref, orb_ref, part, part_in, fields_own, fields_in, send, recv, guest, done, lent,
-    load_sem, aux_sem, part_sem, field_sem, pot_send, pot_recv, orb_send, orb_recv,
+    chol, half, green, gauss_ref, orb_ref, part, part_in, partial, partial_in, bias_ref, log_all, fields_ref,
+    send, recv, guest, done, lent,
+    load_sem, aux_sem, part_sem, sum_sem, field_sem, pot_send, pot_recv, orb_send, orb_recv,
     lend_send, lend_recv, done_send, done_recv,
 ):
     me = lax.axis_index("chol")
-    owned = part.shape[1]
+    owned = orb_ref.shape[0]
     tiles = chol.shape[0]
     width = chol.shape[3]
     nocc = orb_ref.shape[-1]
@@ -232,17 +234,26 @@
     ]
     barrier = pltpu.get_barrier_semaphore()
 
-    def peer_of(k):
-        return lax.rem(me + k, n)
-
-    def greet(k, _):
-        pl.semaphore_signal(
-            barrier, inc=1, device_id={"chol": peer_of(k)}, device_id_type=pl.DeviceIdType.MESH
-        )
-        return 0
-
-    lax.fori_loop(1, n, greet, 0)
-    pl.semaphore_wait(barrier, n - 1)
+    partner = seat + 1 - 2 * lax.rem(seat, 2)
+    beside = lax.rem(seat + 2, PLANE)
+    diagonal = lax.rem(partner + 2, PLANE)
+    others = (beside, diagonal, partner)
+
+    def greet(peer):
+        pl.semaphore_signal(barrier, inc=1, device_id={"chol": peer}, device_id_type=pl.DeviceIdType.MESH)
+
+    greet(ahead * PLANE + seat)
+    for s in others:
+        greet(z * PLANE + s)
+
+    @pl.when(inner)
+    def _():
+        greet(buddy * PLANE + seat)
+        pl.semaphore_wait(barrier, PLANE + 1)
+
+    @pl.when(outer)
+    def _():
+        pl.semaphore_wait(barrier, PLANE)
 
     def at(plane):
         return plane * PLANE + seat
@@ -313,46 +324,68 @@
 
     total = lax.fori_loop(0, tiles, bias, jnp.zeros((n * owned, half.shape[0]), jnp.float32))
     for d in range(n):
-        part[d] = total[d * owned:(d + 1) * owned]
-
-    def push_part(k, _):
-        to = peer_of(k)
-        remote(part.at[to], part_in.at[me], part_sem.at[0], part_sem.at[1], to).start()
-        return 0
-
-    lax.fori_loop(1, n, push_part, 0)
-    start_own(FIRST, SECOND)
+        plane, s = divmod(d, PLANE)
+        part[s, plane * owned:(plane + 1) * owned] = total[d * owned:(d + 1) * owned]
+
+    def part_copy(there, source):
+        return remote(part.at[there], part_in.at[source], part_sem.at[0], part_sem.at[1], z * PLANE + there)
+
+    def field_copy(there):
+        mine = fields_ref.at[seat]
+        return remote(mine, mine, field_sem.at[0], field_sem.at[1], z * PLANE + there)
+
+    def gathered(ref, sem):
+        every = ref.at[pl.ds(0, PLANE - 1)]
+        return remote(every, every, sem.at[0], sem.at[1], at(ahead))
+
+    def sum_copy(k, to):
+        return remote(partial.at[k], partial_in.at[k], sum_sem.at[0, k], sum_sem.at[1, k], to)
+
+    def total_copy():
+        return remote(bias_ref, bias_ref, sum_sem.at[0, 2], sum_sem.at[1, 2], at(buddy))
+
+    for s in others:
+        part_copy(s, seat).start()
+    part_in[seat] = part[seat]
+
+    @pl.when(inner)
+    def _():
+        start_own(FIRST, SECOND)
+
     pass_back(0, FIRST)
-    part_in[me] = part[me]
-
-    def gathered(ref, sem):
-        every = ref.at[pl.ds(0, n - 1)]
-        return remote(every, every, sem.at[0], sem.at[1], peer_of(1))
-
     gathered(part_in, part_sem).wait_recv()
-    vbias = jnp.sum(part_in[...], axis=0)
-    gauss = gauss_ref[me]
+    partial[0] = jnp.sum(part_in[...], axis=0)
+
+    @pl.when(outer)
+    def _():
+        sum_copy(0, at(ahead)).start()
+        start_own(FIRST, chunks)
+        total_copy().wait_recv()
+
+    @pl.when(inner)
+    def _():
+        sum_copy(0, at(ahead)).wait_recv()
+        partial[1] = partial[0] + partial_in[0]
+        sum_copy(1, at(ahead)).start()
+        start_own(SECOND, THIRD)
+        sum_copy(1, at(ahead)).wait_recv()
+        bias_ref[...] = partial[1] + partial_in[1]
+        total_copy().start()
+        start_own(THIRD, chunks)
+
+    pass_back(FIRST, SECOND)
+    vbias = bias_ref[...]
+    gauss = jnp.concatenate([gauss_ref[plane * PLANE + seat] for plane in range(planes)], axis=0)
     xbar = jnp.clip(-0.3 * vbias, -1.0, 1.0)
-    log_ref[...] = jnp.broadcast_to(
-        jnp.sum(gauss * xbar - 0.5 * xbar * xbar, axis=1, keepdims=True), log_ref.shape
-    )
-    mine = gauss - xbar
-    fields_own[...] = mine
-    fields_in[me] = mine
-
-    def push_field(k, _):
-        to = peer_of(k)
-        remote(fields_own, fields_in.at[me], field_sem.at[0], field_sem.at[1], to).start()
-        return 0
-
-    lax.fori_loop(1, n, push_field, 0)
-    start_own(SECOND, chunks)
-    pass_back(FIRST, SECOND)
-
-    gathered(fields_in, field_sem).wait_recv()
-    fields = jnp.concatenate(
-        [fields_in[plane * PLANE + s] for s in range(PLANE) for plane in range(planes)], axis=0
-    ).astype(jnp.bfloat16)
+    logs = jnp.sum(gauss * xbar - 0.5 * xbar * xbar, axis=1, keepdims=True)
+    log_all[...] = jnp.broadcast_to(logs, (line, LANES)).reshape(log_all.shape)
+    log_ref[...] = log_all[z]
+    fields_ref[seat] = (gauss - xbar).astype(jnp.bfloat16)
+
+    for s in others:
+        field_copy(s).start()
+    gathered(fields_ref, field_sem).wait_recv()
+    fields = fields_ref[...].reshape(n * owned, fields_ref.shape[-1])
 
     order = (
         jnp.where(inner, far_in, near_in), jnp.where(inner, far_out, far_in),
@@ -365,11 +398,6 @@
             recv.at[pl.ds(plane * owned, owned), source, t],
             pot_send.at[0], pot_recv.at[plane, source], z * PLANE + there,
         )
-
-    partner = seat + 1 - 2 * lax.rem(seat, 2)
-    beside = lax.rem(seat + 2, PLANE)
-    diagonal = lax.rem(partner + 2, PLANE)
-    others = (beside, diagonal, partner)
 
     def push(t, plane):
         for s in others:
@@ -501,12 +529,21 @@
             lax.fori_loop(0, owned, borrow, 0)
 
     gathered(part_in, part_sem).wait_send()
-    gathered(fields_in, field_sem).wait_send()
+    gathered(fields_ref, field_sem).wait_send()
     every = send.at[:, pl.ds(0, (PLANE - 1) * line)]
     remote(every, every, pot_send.at[0], pot_recv.at[z, seat], at(ahead)).wait_send()
 
     def sent(ref, sem):
         remote(ref, ref, sem, lend_recv.at[0], at(ahead)).wait_send()
+
+    @pl.when(outer)
+    def _():
+        sum_copy(0, at(ahead)).wait_send()
+
+    @pl.when(inner)
+    def _():
+        sum_copy(1, at(ahead)).wait_send()
+        total_copy().wait_send()
 
     sent(orb_ref, orb_send.at[0])
 
@@ -548,13 +585,6 @@
         pltpu.VMEM((vectors, local_rows, nocc), jnp.bfloat16),
         pltpu.VMEM((walkers, local_rows, nocc), jnp.bfloat16),
     ]
-    sums = [
-        pltpu.VMEM((n, owned, vectors), jnp.float32),
-        pltpu.VMEM((n, owned, vectors), jnp.float32),
-        pltpu.VMEM((owned, vectors), jnp.float32),
-        pltpu.VMEM((n, owned, vectors), jnp.float32),
-        pltpu.VMEM((tiles, walkers, TILE, width), jnp.bfloat16),
-    ]
     arrays = (chol_full, chol_half, green, gauss.reshape(n, owned, vectors), orbitals.reshape(split))
     if n == 4 * PLANE and orbitals.size * orbitals.dtype.itemsize <= OWN_LIMIT:
         line = walkers // PLANE
@@ -568,12 +598,19 @@
                 *shared,
                 pltpu.VMEM((n, owned, vectors), jnp.float32),
                 pltpu.VMEM(split, jnp.bfloat16),
-                *sums,
+                pltpu.VMEM((PLANE, line, vectors), jnp.float32),
+                pltpu.VMEM((PLANE, line, vectors), jnp.float32),
+                pltpu.VMEM((2, line, vectors), jnp.float32),
+                pltpu.VMEM((2, line, vectors), jnp.float32),
+                pltpu.VMEM((line, vectors), jnp.float32),
+                pltpu.VMEM((planes, owned, LANES), jnp.float32),
+                pltpu.VMEM((PLANE, line, vectors), jnp.bfloat16),
+                pltpu.VMEM((tiles, walkers, TILE, width), jnp.bfloat16),
                 pltpu.VMEM((line, PLANE, tiles, TILE, width), jnp.bfloat16),
                 pltpu.VMEM((planes,) + split, jnp.bfloat16),
                 pltpu.VMEM((line, PLANE, tiles, TILE, nocc), jnp.bfloat16),
                 pltpu.VMEM((owned, PLANE, tiles, TILE, width), jnp.bfloat16),
-                dma((tiles,)), dma((4,)), dma((2,)), dma((2,)), dma((1,)), dma((planes, PLANE)),
+                dma((tiles,)), dma((4,)), dma((2,)), dma((2, 3)), dma((2,)), dma((1,)), dma((planes, PLANE)),
                 dma((4,)), dma((planes, CHUNKS * owned)), dma((1,)), dma((PLANE,)), dma((planes,)), dma((planes,)),
             ],
             compiler_params=params,
@@ -589,7 +626,11 @@
             out_specs=(vmem, vmem),
             scratch_shapes=[
                 *shared,
-                *sums,
+                pltpu.VMEM((n, owned, vectors), jnp.float32),
+                pltpu.VMEM((n, owned, vectors), jnp.float32),
+                pltpu.VMEM((owned, vectors), jnp.float32),
+                pltpu.VMEM((n, owned, vectors), jnp.float32),
+                pltpu.VMEM((tiles, walkers, TILE, width), jnp.bfloat16),
                 pltpu.VMEM((tiles, owned, n * TILE, width), jnp.bfloat16),
                 dma((tiles,)), dma((2,)), dma((n,)), dma((n,)), dma((n,)), dma((n,)),
                 dma((tiles, n)), dma((tiles, n)),

time: 147 us -> 145 us (0.986)
  Pallas kernels: 145 us -> 142 us
    pallas_call x1, Pallas kernels: 145 us -> 142 us  [on_device(): pl.pallas_call(functools.partial(line_kernel, n), out_shape=(pltpu.VMEM(s...]
where the time goes in v5:
time: 145 us
  Pallas kernels  142 us (98%)
  local copies, waits for them, and re-layouts  1.95 us (1%)
    pallas_call x1, Pallas kernels, on_device(): pl.pallas_call(functools.partial(line_kernel, n), out_shape=(pltpu.VMEM(s...  142 us

profile of v5, /device:TPU:0, one launch (start us, length us, event | category | flops | bytes accessed | tf_op | source)
XLA Modules:
  0.0 145.0 jit_solution(9968033734526376753)
XLA Ops:
  0.6 142.4 %shard_map.68 = (bf16[4,16,4,16,256]{4,3,2,1,0:T(8,128)(2,1)S(1)}, f32[4,128]{1,0:T(4,128)S(1)}) custom-call(bf16[128,64,1024]{2,1,0:T(8,128)(2,1)} %chol_hbm.1, bf16[128,64,256]{2,1,0:T(8,128)(2,1)} %half_hbm.1, bf16[64,64,256]{2,1,0:T(8,128)(2,1)} %green_hbm.1, f32[16,4,128]{2,1,0:T(4,128)} %bitcast.5, bf16[4,16,4,16,256]{4,3,2,1,0:T(8,128)(2,1)} %bitcast.4), custom_call_target="tpu_custom_call" | custom-call | tf_op jit(solution)/shard_map/pallas_call | solution.py:592
  143.0 1.3 copy.8
  144.3 0.6 slice_reduce_fusion

commit v6 on v5

--- a/solution.py
+++ b/solution.py
@@ -199,7 +199,7 @@
     chol, half, green, gauss_ref, orb_ref, part, part_in, partial, partial_in, bias_ref, log_all, fields_ref,
     send, recv, guest, done, lent,
     load_sem, aux_sem, part_sem, sum_sem, field_sem, pot_send, pot_recv, orb_send, orb_recv,
-    lend_send, lend_recv, done_send, done_recv,
+    lend_sem, done_sem,
 ):
     me = lax.axis_index("chol")
     owned = orb_ref.shape[0]
@@ -226,10 +226,10 @@
     green_copy = pltpu.make_async_copy(green_hbm, green, aux_sem.at[1])
     gauss_copy = pltpu.make_async_copy(gauss_hbm, gauss_ref, aux_sem.at[2])
     orb_copy = pltpu.make_async_copy(orb_hbm, orb_ref, aux_sem.at[3])
-    for copy in (orb_copy, green_copy, half_copy, gauss_copy):
+    for copy in (green_copy, half_copy, gauss_copy):
         copy.start()
     loads = [
-        pltpu.make_async_copy(chol_hbm.at[:, pl.ds(t * TILE, TILE), :], chol.at[t], load_sem.at[t])
+        pltpu.make_async_copy(chol_hbm.at[:, pl.ds(t * TILE, TILE), :], chol.at[t], load_sem.at[0])
         for t in range(tiles)
     ]
     barrier = pltpu.get_barrier_semaphore()
@@ -261,20 +261,25 @@
     def piece(ref, c):
         return ref.at[c // CHUNKS, pl.ds(lax.rem(c, CHUNKS) * span, span)]
 
+    def landed(plane, to, c):
+        return orb_recv.at[lax.rem(plane - to + planes, planes) - 1, c]
+
     def own_orbit(c):
-        return remote(piece(orb_ref, c), piece(guest.at[z], c), orb_send.at[0], orb_recv.at[z, c], at(ahead))
+        return remote(piece(orb_hbm, c), piece(guest.at[z], c), orb_send.at[0], landed(z, ahead, c), at(ahead))
+
+    def orbit_copy(plane, to, c):
+        there = piece(guest.at[plane], c)
+        return remote(there, there, orb_send.at[0], landed(plane, to, c), at(to))
 
     def orbit_on(c):
-        there = piece(guest.at[near_out], c)
-        return remote(there, there, orb_send.at[1], orb_recv.at[near_out, c], at(ahead))
-
-    def orbit_back(plane, k, c):
-        there = piece(guest.at[plane], c)
-        return remote(there, there, orb_send.at[k], orb_recv.at[plane, c], at(buddy))
+        return orbit_copy(near_out, ahead, c)
+
+    def orbit_back(plane, c):
+        return orbit_copy(plane, buddy, c)
 
     def await_orbit(plane, c):
         there = piece(guest.at[plane], c)
-        remote(there, there, orb_send.at[0], orb_recv.at[plane, c], at(ahead)).wait_recv()
+        remote(there, there, orb_send.at[0], landed(plane, z, c), at(ahead)).wait_recv()
 
     def start_own(first, last):
         def step(c, _):
@@ -298,18 +303,17 @@
         def _():
             def step(c, _):
                 await_orbit(far_in, c)
-                orbit_back(far_in, 2, c).start()
+                orbit_back(far_in, c).start()
                 return 0
 
             lax.fori_loop(first, last, step, 0)
 
-    orb_copy.wait()
     start_own(0, FIRST)
 
     half_copy.wait()
     green_copy.wait()
-    for load in loads:
-        load.start()
+    for copy in (*loads, orb_copy):
+        copy.start()
     gauss_copy.wait()
 
     def bias(t, acc):
@@ -339,10 +343,10 @@
         return remote(every, every, sem.at[0], sem.at[1], at(ahead))
 
     def sum_copy(k, to):
-        return remote(partial.at[k], partial_in.at[k], sum_sem.at[0, k], sum_sem.at[1, k], to)
+        return remote(partial.at[k], partial_in.at[k], sum_sem.at[0, 0], sum_sem.at[1, k], to)
 
     def total_copy():
-        return remote(bias_ref, bias_ref, sum_sem.at[0, 2], sum_sem.at[1, 2], at(buddy))
+        return remote(bias_ref, bias_ref, sum_sem.at[0, 1], sum_sem.at[1, 0], at(buddy))
 
     for s in others:
         part_copy(s, seat).start()
@@ -385,6 +389,7 @@
     for s in others:
         field_copy(s).start()
     gathered(fields_ref, field_sem).wait_recv()
+    pltpu.make_async_copy(chol, chol, load_sem.at[0]).wait()
     fields = fields_ref[...].reshape(n * owned, fields_ref.shape[-1])
 
     order = (
@@ -396,21 +401,18 @@
         return remote(
             send.at[t, pl.ds(there * line + plane * owned, owned)],
             recv.at[pl.ds(plane * owned, owned), source, t],
-            pot_send.at[0], pot_recv.at[plane, source], z * PLANE + there,
+            pot_send.at[0], pot_recv.at[plane], z * PLANE + there,
         )
 
     def push(t, plane):
         for s in others:
             pot_copy(t, plane, s, seat).start()
 
-    def await_pots(plane, seats):
-        for s in seats:
-            every = recv.at[pl.ds(plane * owned, owned), s]
-            remote(every, every, pot_send.at[0], pot_recv.at[plane, s], z * PLANE + partner).wait_recv()
+    def await_pots(plane):
+        every = recv.at[pl.ds(plane * owned, owned), pl.ds(0, PLANE - 1)]
+        remote(every, every, pot_send.at[0], pot_recv.at[plane], z * PLANE + partner).wait_recv()
 
     def fill(t):
-        loads[t].wait()
-
         def strip(c, _):
             cols = pl.ds(pl.multiple_of(c * LANES, LANES), LANES)
             block = jnp.swapaxes(chol[t, :, :, cols], 0, 1)
@@ -430,7 +432,7 @@
 
             @pl.when(inner)
             def _():
-                orbit_back(far_out, 3, c).start()
+                orbit_back(far_out, c).start()
 
             return 0
 
@@ -446,10 +448,8 @@
         for t in range(tiles):
             push(t, plane)
 
-    def lend(s):
-        return remote(
-            recv.at[pl.ds(buddy * owned, owned), s], lent.at[:, s], lend_send.at[0], lend_recv.at[s], at(buddy)
-        )
+    def lend():
+        return remote(recv.at[pl.ds(buddy * owned, owned)], lent, lend_sem.at[0], lend_sem.at[1], at(buddy))
 
     pass_on(0, held + 1)
     pass_back(held, held + 2)
@@ -458,10 +458,8 @@
     pass_on(held + 2, chunks)
     @pl.when(outer)
     def _():
-        lend(seat).start()
-        for s in (partner, beside, diagonal):
-            await_pots(near_in, (s,))
-            lend(s).start()
+        await_pots(near_in)
+        lend().start()
 
         def arrived(c, _):
             await_orbit(far_in, c)
@@ -472,7 +470,7 @@
     def hand_back(plane, w):
         return remote(
             done.at[plane * owned + w], out_ref.at[w, pl.ds(z * PLANE, PLANE)],
-            done_send.at[plane], done_recv.at[z], at(plane),
+            done_sem.at[0], done_sem.at[1], at(plane),
         )
 
     def rows_done(left, orbit, old):
@@ -494,10 +492,13 @@
         lax.fori_loop(first, last, step, 0)
 
     forward_far(0, CHUNKS)
-    await_pots(far_in, others)
-    serve(far_in, 0, owned)
+    await_pots(far_in)
+    @pl.when(outer)
+    def _():
+        serve(far_in, 0, owned)
+
     forward_far(CHUNKS, 2 * CHUNKS)
-    await_pots(far_out, others)
+    await_pots(far_out)
     serve(far_out, 0, 2)
     for w in range(2, owned):
         forward_far(CHUNKS * w, CHUNKS * (w + 1))
@@ -505,10 +506,15 @@
 
     @pl.when(inner)
     def _():
-        await_pots(near_out, others)
+        serve(far_in, 0, owned)
+
+    @pl.when(inner)
+    def _():
+        await_pots(near_out)
         serve(near_out, 0, owned)
 
-    await_pots(z, others)
+    await_pots(z)
+    orb_copy.wait()
 
     def advance(w, _):
         out_ref[w, here] = rows_done(recv[z * owned + w], orb_ref[w], orb_ref[w, here])
@@ -518,56 +524,57 @@
 
     @pl.when(inner)
     def _():
-        for s in (seat, partner, beside, diagonal):
-            lend(s).wait_recv()
-
-            def borrow(w, _):
-                row = near_out * PLANE + s
-                out_ref[w, row] = rows_done(lent[w, s], orb_ref[w], orb_ref[w, row])
-                return 0
-
-            lax.fori_loop(0, owned, borrow, 0)
+        lend().wait_recv()
+        there = pl.ds(near_out * PLANE, PLANE)
+
+        def borrow(w, _):
+            out_ref[w, there] = rows_done(lent[w], orb_ref[w], orb_ref[w, there])
+            return 0
+
+        lax.fori_loop(0, owned, borrow, 0)
 
     gathered(part_in, part_sem).wait_send()
     gathered(fields_ref, field_sem).wait_send()
     every = send.at[:, pl.ds(0, (PLANE - 1) * line)]
-    remote(every, every, pot_send.at[0], pot_recv.at[z, seat], at(ahead)).wait_send()
-
-    def sent(ref, sem):
-        remote(ref, ref, sem, lend_recv.at[0], at(ahead)).wait_send()
+    remote(every, every, pot_send.at[0], pot_recv.at[z], at(ahead)).wait_send()
+
+    def through(ref, sem):
+        return remote(ref, ref, sem.at[0], sem.at[1], at(ahead))
 
     @pl.when(outer)
     def _():
         sum_copy(0, at(ahead)).wait_send()
+        lend().wait_send()
+        remote(guest.at[0], guest.at[0], orb_send.at[0], orb_recv.at[0, 0], at(ahead)).wait_send()
+        through(done.at[pl.ds(0, 2 * owned)], done_sem).wait_send()
 
     @pl.when(inner)
     def _():
         sum_copy(1, at(ahead)).wait_send()
         total_copy().wait_send()
-
-    sent(orb_ref, orb_send.at[0])
-
-    @pl.when(inner)
-    def _():
-        for k in range(1, 4):
-            sent(guest.at[0], orb_send.at[k])
-        sent(done.at[pl.ds(0, owned)], done_send.at[near_out])
+        remote(guest, guest, orb_send.at[0], orb_recv.at[0, 0], at(ahead)).wait_send()
+        through(done.at[pl.ds(0, 3 * owned)], done_sem).wait_send()
 
     @pl.when(outer)
     def _():
-        sent(lent, lend_send.at[0])
-
-    def settle(plane):
-        block = out_ref.at[:, pl.ds(plane * PLANE, PLANE)]
-        remote(block, block, done_send.at[plane], done_recv.at[plane], at(plane)).wait_recv()
-
-    for plane in (far_in, far_out):
-        sent(done.at[pl.ds(0, owned)], done_send.at[plane])
-        settle(plane)
-
-    @pl.when(outer)
-    def _():
-        settle(near_in)
+        through(out_ref.at[:, pl.ds(0, 3 * PLANE)], done_sem).wait_recv()
+
+    @pl.when(inner)
+    def _():
+        through(out_ref.at[:, pl.ds(0, 2 * PLANE)], done_sem).wait_recv()
+
+
+def close_kernel(moved_ref, logs_ref, out_hbm, log_hbm, log_ref, sem):
+    copies = [
+        pltpu.make_async_copy(moved_ref.at[w], out_hbm.at[w], sem.at[w]) for w in range(moved_ref.shape[0])
+    ]
+    for copy in copies:
+        copy.start()
+    log_ref[...] = logs_ref[:, 0]
+    copies.append(pltpu.make_async_copy(log_ref, log_hbm, sem.at[len(copies)]))
+    copies[-1].start()
+    for copy in copies:
+        copy.wait()
 
 
 def on_device(n, chol_full, chol_half, green, gauss, orbitals):
@@ -610,11 +617,23 @@
                 pltpu.VMEM((planes,) + split, jnp.bfloat16),
                 pltpu.VMEM((line, PLANE, tiles, TILE, nocc), jnp.bfloat16),
                 pltpu.VMEM((owned, PLANE, tiles, TILE, width), jnp.bfloat16),
-                dma((tiles,)), dma((4,)), dma((2,)), dma((2, 3)), dma((2,)), dma((1,)), dma((planes, PLANE)),
-                dma((4,)), dma((planes, CHUNKS * owned)), dma((1,)), dma((PLANE,)), dma((planes,)), dma((planes,)),
+                dma((1,)), dma((4,)), dma((2,)), dma((2, 2)), dma((2,)), dma((1,)), dma((planes,)),
+                dma((1,)), dma((planes - 1, CHUNKS * owned)), dma((2,)), dma((2,)),
             ],
             compiler_params=params,
         )(*arrays)
+        moved, logs = pl.pallas_call(
+            close_kernel,
+            out_shape=(
+                jax.ShapeDtypeStruct(split, jnp.bfloat16),
+                jax.ShapeDtypeStruct((owned,), jnp.float32),
+            ),
+            in_specs=[pl.BlockSpec(memory_space=pltpu.VMEM)] * 2,
+            out_specs=(hbm, hbm),
+            scratch_shapes=[pltpu.VMEM((owned,), jnp.float32), dma((owned + 1,))],
+            compiler_params=pltpu.CompilerParams(vmem_limit_bytes=1 << 20),
+        )(moved, logs)
+        return moved.reshape(orbitals.shape), logs
     else:
         moved, logs = pl.pallas_call(
             functools.partial(direct_kernel, n),

time: 145 us -> 143 us (0.986)
  local copies, waits for them, and re-layouts: 1.95 us -> 0 us
where the time goes in v6:
time: 143 us
  Pallas kernels  142 us (99%)
    pallas_call x1, Pallas kernels, on_device(): pl.pallas_call(functools.partial(line_kernel, n), out_shape=(pltpu.VMEM(s...  141 us

profile of v6, /device:TPU:0, one launch (start us, length us, event | category | flops | bytes accessed | tf_op | source)
XLA Modules:
  0.0 143.1 jit_solution(14861686718293260337)
XLA Ops:
  0.6 141.1 %shard_map.68 = (bf16[4,16,4,16,256]{4,3,2,1,0:T(8,128)(2,1)S(1)}, f32[4,128]{1,0:T(4,128)S(1)}) custom-call(bf16[128,64,1024]{2,1,0:T(8,128)(2,1)} %chol_hbm.1, bf16[128,64,256]{2,1,0:T(8,128)(2,1)} %half_hbm.1, bf16[64,64,256]{2,1,0:T(8,128)(2,1)} %green_hbm.1, f32[16,4,128]{2,1,0:T(4,128)} %bitcast.4, bf16[4,16,4,16,256]{4,3,2,1,0:T(8,128)(2,1)} %bitcast.3), custom_call_target="tpu_custom_call" | custom-call | tf_op jit(solution)/shard_map/pallas_call | solution.py:599
  141.7 1.4 shard_map.69

commit v7 on v6

--- a/solution.py
+++ b/solution.py
@@ -199,7 +199,7 @@
     chol, half, green, gauss_ref, orb_ref, part, part_in, partial, partial_in, bias_ref, log_all, fields_ref,
     send, recv, guest, done, lent,
     load_sem, aux_sem, part_sem, sum_sem, field_sem, pot_send, pot_recv, orb_send, orb_recv,
-    lend_sem, done_sem,
+    lend_sem, done_sem, news, ready,
 ):
     me = lax.axis_index("chol")
     owned = orb_ref.shape[0]
@@ -222,6 +222,29 @@
     inner = z == near_in
     outer = z == near_out
 
+    barrier = pltpu.get_barrier_semaphore()
+
+    partner = seat + 1 - 2 * lax.rem(seat, 2)
+    beside = lax.rem(seat + 2, PLANE)
+    diagonal = lax.rem(partner + 2, PLANE)
+    others = (beside, diagonal, partner)
+
+    def greet(peer):
+        pl.semaphore_signal(barrier, inc=1, device_id={"chol": peer}, device_id_type=pl.DeviceIdType.MESH)
+
+    def tell(sem, peer):
+        pl.semaphore_signal(sem, inc=1, device_id={"chol": peer}, device_id_type=pl.DeviceIdType.MESH)
+
+    @pl.when(inner)
+    def _():
+        greet(ahead * PLANE + seat)
+        greet(buddy * PLANE + seat)
+
+    @pl.when(outer)
+    def _():
+        for s in others:
+            greet(z * PLANE + s)
+
     half_copy = pltpu.make_async_copy(half_hbm, half, aux_sem.at[0])
     green_copy = pltpu.make_async_copy(green_hbm, green, aux_sem.at[1])
     gauss_copy = pltpu.make_async_copy(gauss_hbm, gauss_ref, aux_sem.at[2])
@@ -232,28 +255,15 @@
         pltpu.make_async_copy(chol_hbm.at[:, pl.ds(t * TILE, TILE), :], chol.at[t], load_sem.at[0])
         for t in range(tiles)
     ]
-    barrier = pltpu.get_barrier_semaphore()
-
-    partner = seat + 1 - 2 * lax.rem(seat, 2)
-    beside = lax.rem(seat + 2, PLANE)
-    diagonal = lax.rem(partner + 2, PLANE)
-    others = (beside, diagonal, partner)
-
-    def greet(peer):
-        pl.semaphore_signal(barrier, inc=1, device_id={"chol": peer}, device_id_type=pl.DeviceIdType.MESH)
-
-    greet(ahead * PLANE + seat)
-    for s in others:
-        greet(z * PLANE + s)
-
-    @pl.when(inner)
-    def _():
-        greet(buddy * PLANE + seat)
-        pl.semaphore_wait(barrier, PLANE + 1)
+    @pl.when(inner)
+    def _():
+        pl.semaphore_wait(barrier, 1)
 
     @pl.when(outer)
     def _():
         pl.semaphore_wait(barrier, PLANE)
+        for s in others:
+            tell(news, z * PLANE + s)
 
     def at(plane):
         return plane * PLANE + seat
@@ -309,6 +319,12 @@
             lax.fori_loop(first, last, step, 0)
 
     start_own(0, FIRST)
+
+    @pl.when(outer)
+    def _():
+        pl.semaphore_wait(news, PLANE - 1)
+        tell(ready, at(ahead))
+
 
     half_copy.wait()
     green_copy.wait()
@@ -330,6 +346,10 @@
     for d in range(n):
         plane, s = divmod(d, PLANE)
         part[s, plane * owned:(plane + 1) * owned] = total[d * owned:(d + 1) * owned]
+
+    @pl.when(inner)
+    def _():
+        pl.semaphore_wait(ready, 1)
 
     def part_copy(there, source):
         return remote(part.at[there], part_in.at[source], part_sem.at[0], part_sem.at[1], z * PLANE + there)
@@ -619,6 +639,7 @@
                 pltpu.VMEM((owned, PLANE, tiles, TILE, width), jnp.bfloat16),
                 dma((1,)), dma((4,)), dma((2,)), dma((2, 2)), dma((2,)), dma((1,)), dma((planes,)),
                 dma((1,)), dma((planes - 1, CHUNKS * owned)), dma((2,)), dma((2,)),
+                pltpu.SemaphoreType.REGULAR, pltpu.SemaphoreType.REGULAR,
             ],
             compiler_params=params,
         )(*arrays)

time: 143 us -> 141 us (0.986)
    pallas_call x1, Pallas kernels: 141 us -> 139 us  [on_device(): pl.pallas_call(functools.partial(line_kernel, n), out_shape=(pltpu.VMEM(s...]
where the time goes in v7:
time: 141 us
  Pallas kernels  141 us (100%)
    pallas_call x1, Pallas kernels, on_device(): pl.pallas_call(functools.partial(line_kernel, n), out_shape=(pltpu.VMEM(s...  139 us

profile of v7, /device:TPU:0, one launch (start us, length us, event | category | flops | bytes accessed | tf_op | source)
XLA Modules:
  0.0 141.3 jit_solution(15837619323211314587)
XLA Ops:
  0.6 139.3 %shard_map.68 = (bf16[4,16,4,16,256]{4,3,2,1,0:T(8,128)(2,1)S(1)}, f32[4,128]{1,0:T(4,128)S(1)}) custom-call(bf16[128,64,1024]{2,1,0:T(8,128)(2,1)} %chol_hbm.1, bf16[128,64,256]{2,1,0:T(8,128)(2,1)} %half_hbm.1, bf16[64,64,256]{2,1,0:T(8,128)(2,1)} %green_hbm.1, f32[16,4,128]{2,1,0:T(4,128)} %bitcast.4, bf16[4,16,4,16,256]{4,3,2,1,0:T(8,128)(2,1)} %bitcast.3), custom_call_target="tpu_custom_call" | custom-call | tf_op jit(solution)/shard_map/pallas_call | solution.py:619
  140.0 1.4 shard_map.69

commit v8 on v7

--- a/solution.py
+++ b/solution.py
@@ -461,9 +461,9 @@
     for t in range(tiles):
         fill(t)
         push(t, order[0])
-        if t < tiles - 2:
+        if t < tiles - 1:
             pass_back(SECOND + t, SECOND + t + 1)
-    held = SECOND + tiles - 2
+    held = SECOND + tiles - 1
     for plane in order[1:]:
         for t in range(tiles):
             push(t, plane)
@@ -471,8 +471,9 @@
     def lend():
         return remote(recv.at[pl.ds(buddy * owned, owned)], lent, lend_sem.at[0], lend_sem.at[1], at(buddy))
 
+    pass_back(held, held + 1)
     pass_on(0, held + 1)
-    pass_back(held, held + 2)
+    pass_back(held + 1, held + 2)
     pass_on(held + 1, held + 2)
     pass_back(held + 2, chunks)
     pass_on(held + 2, chunks)

time: 141 us -> 141 us (level)
  no operation moved by 1% of the time
where the time goes in v8:
time: 141 us
  Pallas kernels  140 us (99%)
    pallas_call x1, Pallas kernels, on_device(): pl.pallas_call(functools.partial(line_kernel, n), out_shape=(pltpu.VMEM(s...  139 us

profile of v8, /device:TPU:0, one launch (start us, length us, event | category | flops | bytes accessed | tf_op | source)
XLA Modules:
  0.0 140.5 jit_solution(2703046528698224178)
XLA Ops:
  0.6 138.5 %shard_map.68 = (bf16[4,16,4,16,256]{4,3,2,1,0:T(8,128)(2,1)S(1)}, f32[4,128]{1,0:T(4,128)S(1)}) custom-call(bf16[128,64,1024]{2,1,0:T(8,128)(2,1)} %chol_hbm.1, bf16[128,64,256]{2,1,0:T(8,128)(2,1)} %half_hbm.1, bf16[64,64,256]{2,1,0:T(8,128)(2,1)} %green_hbm.1, f32[16,4,128]{2,1,0:T(4,128)} %bitcast.4, bf16[4,16,4,16,256]{4,3,2,1,0:T(8,128)(2,1)} %bitcast.3), custom_call_target="tpu_custom_call" | custom-call | tf_op jit(solution)/shard_map/pallas_call | solution.py:620
  139.1 1.4 shard_map.69

commit v9 on v7

--- a/solution.py
+++ b/solution.py
@@ -11,10 +11,10 @@
 LANES = 128
 PLANE = 4
 OWN_LIMIT = 2 << 20
-CHUNKS = 2
-FIRST = 1
-SECOND = 2
-THIRD = 3
+CHUNKS = 4
+FIRST = 2
+SECOND = 4
+THIRD = 6
 
 
 def remote(src, dst, send, recv, peer):
@@ -392,12 +392,13 @@
         partial[1] = partial[0] + partial_in[0]
         sum_copy(1, at(ahead)).start()
         start_own(SECOND, THIRD)
+        pass_back(FIRST, FIRST + 1)
         sum_copy(1, at(ahead)).wait_recv()
         bias_ref[...] = partial[1] + partial_in[1]
         total_copy().start()
         start_own(THIRD, chunks)
 
-    pass_back(FIRST, SECOND)
+    pass_back(FIRST + 1, SECOND)
     vbias = bias_ref[...]
     gauss = jnp.concatenate([gauss_ref[plane * PLANE + seat] for plane in range(planes)], axis=0)
     xbar = jnp.clip(-0.3 * vbias, -1.0, 1.0)
@@ -443,7 +444,10 @@
             send[t, :, :, cols] = jnp.swapaxes(jnp.stack(pots, axis=0), 0, 1)
             return 0
 
-        lax.fori_loop(0, width // LANES, strip, 0)
+        half_way = width // LANES // 2
+        lax.fori_loop(0, half_way, strip, 0)
+        pass_back(SECOND + 2 * t, SECOND + 2 * t + 1)
+        lax.fori_loop(half_way, width // LANES, strip, 0)
         recv[:, seat, t] = send[t, pl.ds(seat * line, line)]
 
     def forward_far(first, last):
@@ -461,9 +465,9 @@
     for t in range(tiles):
         fill(t)
         push(t, order[0])
-        if t < tiles - 2:
-            pass_back(SECOND + t, SECOND + t + 1)
-    held = SECOND + tiles - 2
+        pass_back(SECOND + 2 * t + 1, SECOND + 2 * t + 2)
+    held = SECOND + 2 * tiles
+
     for plane in order[1:]:
         for t in range(tiles):
             push(t, plane)
@@ -471,11 +475,10 @@
     def lend():
         return remote(recv.at[pl.ds(buddy * owned, owned)], lent, lend_sem.at[0], lend_sem.at[1], at(buddy))
 
-    pass_on(0, held + 1)
-    pass_back(held, held + 2)
-    pass_on(held + 1, held + 2)
-    pass_back(held + 2, chunks)
-    pass_on(held + 2, chunks)
+    pass_on(0, held)
+    for c in range(held, chunks):
+        pass_back(c, c + 1)
+        pass_on(c, c + 1)
     @pl.when(outer)
     def _():
         await_pots(near_in)

time: 141 us -> 141 us (level); the launches traced: 141 us -> 139 us
  Pallas kernels: 141 us -> 138 us
    pallas_call x1, Pallas kernels: 139 us -> 137 us  [on_device(): pl.pallas_call(functools.partial(line_kernel, n), out_shape=(pltpu.VMEM(s...]
where the time goes in v9:
time: 141 us; the launch traced here: 139 us
  Pallas kernels  138 us (98%)
    pallas_call x1, Pallas kernels, on_device(): pl.pallas_call(functools.partial(line_kernel, n), out_shape=(pltpu.VMEM(s...  137 us

profile of v9, /device:TPU:0, one launch (start us, length us, event | category | flops | bytes accessed | tf_op | source)
XLA Modules:
  0.0 138.8 jit_solution(7443910351891648639)
XLA Ops:
  0.6 136.8 %shard_map.68 = (bf16[4,16,4,16,256]{4,3,2,1,0:T(8,128)(2,1)S(1)}, f32[4,128]{1,0:T(4,128)S(1)}) custom-call(bf16[128,64,1024]{2,1,0:T(8,128)(2,1)} %chol_hbm.1, bf16[128,64,256]{2,1,0:T(8,128)(2,1)} %half_hbm.1, bf16[64,64,256]{2,1,0:T(8,128)(2,1)} %green_hbm.1, f32[16,4,128]{2,1,0:T(4,128)} %bitcast.4, bf16[4,16,4,16,256]{4,3,2,1,0:T(8,128)(2,1)} %bitcast.3), custom_call_target="tpu_custom_call" | custom-call | tf_op jit(solution)/shard_map/pallas_call | solution.py:622
  137.4 1.4 shard_map.69

commit v10 on v9

--- a/solution.py
+++ b/solution.py
@@ -12,6 +12,7 @@
 PLANE = 4
 OWN_LIMIT = 2 << 20
 CHUNKS = 4
+HALVES = 2
 FIRST = 2
 SECOND = 4
 THIRD = 6
@@ -198,7 +199,7 @@
     out_ref, log_ref,
     chol, half, green, gauss_ref, orb_ref, part, part_in, partial, partial_in, bias_ref, log_all, fields_ref,
     send, recv, guest, done, lent,
-    load_sem, aux_sem, part_sem, sum_sem, field_sem, pot_send, pot_recv, orb_send, orb_recv,
+    load_sem, aux_sem, part_sem, sum_sem, field_sem, pot_send, pot_recv, orb_send, orb_recv, half_recv,
     lend_sem, done_sem, news, ready,
 ):
     me = lax.axis_index("chol")
@@ -209,7 +210,6 @@
     planes = n // PLANE
     line = planes * owned
     chunks = CHUNKS * owned
-    span = n // CHUNKS
 
     z = me // PLANE
     seat = lax.rem(me, PLANE)
@@ -268,32 +268,29 @@
     def at(plane):
         return plane * PLANE + seat
 
-    def piece(ref, c):
-        return ref.at[c // CHUNKS, pl.ds(lax.rem(c, CHUNKS) * span, span)]
-
-    def landed(plane, to, c):
-        return orb_recv.at[lax.rem(plane - to + planes, planes) - 1, c]
-
-    def own_orbit(c):
-        return remote(piece(orb_hbm, c), piece(guest.at[z], c), orb_send.at[0], landed(z, ahead, c), at(ahead))
-
-    def orbit_copy(plane, to, c):
-        there = piece(guest.at[plane], c)
-        return remote(there, there, orb_send.at[0], landed(plane, to, c), at(to))
-
-    def orbit_on(c):
-        return orbit_copy(near_out, ahead, c)
-
-    def orbit_back(plane, c):
-        return orbit_copy(plane, buddy, c)
-
-    def await_orbit(plane, c):
-        there = piece(guest.at[plane], c)
-        remote(there, there, orb_send.at[0], landed(plane, z, c), at(ahead)).wait_recv()
-
-    def start_own(first, last):
+    def piece(ref, c, parts):
+        span = n // parts
+        return ref.at[c // parts, pl.ds(lax.rem(c, parts) * span, span)]
+
+    def own_inner(c):
+        there = piece(guest.at[z], c, CHUNKS)
+        return remote(piece(orb_hbm, c, CHUNKS), there, orb_send.at[0], orb_recv.at[c], at(ahead))
+
+    def own_outer(c):
+        there = piece(guest.at[z], c, HALVES)
+        return remote(piece(orb_hbm, c, HALVES), there, orb_send.at[0], half_recv.at[1, c], at(ahead))
+
+    def inner_orbit(c):
+        there = piece(guest.at[far_in], c, CHUNKS)
+        return remote(there, there, orb_send.at[0], orb_recv.at[c], at(buddy))
+
+    def outer_orbit(plane, k, to, c):
+        there = piece(guest.at[plane], c, HALVES)
+        return remote(there, there, orb_send.at[0], half_recv.at[k, c], at(to))
+
+    def start_own(first, last, copy=own_inner):
         def step(c, _):
-            own_orbit(c).start()
+            copy(c).start()
             return 0
 
         lax.fori_loop(first, last, step, 0)
@@ -302,8 +299,8 @@
         @pl.when(inner)
         def _():
             def step(c, _):
-                await_orbit(near_out, c)
-                orbit_on(c).start()
+                outer_orbit(near_out, 1, ahead, c).wait_recv()
+                outer_orbit(near_out, 0, ahead, c).start()
                 return 0
 
             lax.fori_loop(first, last, step, 0)
@@ -312,16 +309,19 @@
         @pl.when(inner)
         def _():
             def step(c, _):
-                await_orbit(far_in, c)
-                orbit_back(far_in, c).start()
+                inner_orbit(c).wait_recv()
+                inner_orbit(c).start()
                 return 0
 
             lax.fori_loop(first, last, step, 0)
 
-    start_own(0, FIRST)
+    @pl.when(inner)
+    def _():
+        start_own(0, FIRST)
 
     @pl.when(outer)
     def _():
+        start_own(0, 1, own_outer)
         pl.semaphore_wait(news, PLANE - 1)
         tell(ready, at(ahead))
 
@@ -383,7 +383,7 @@
     @pl.when(outer)
     def _():
         sum_copy(0, at(ahead)).start()
-        start_own(FIRST, chunks)
+        start_own(1, HALVES * owned, own_outer)
         total_copy().wait_recv()
 
     @pl.when(inner)
@@ -452,11 +452,11 @@
 
     def forward_far(first, last):
         def step(c, _):
-            await_orbit(far_out, c)
+            outer_orbit(far_out, 0, buddy, c).wait_recv()
 
             @pl.when(inner)
             def _():
-                orbit_back(far_out, c).start()
+                outer_orbit(far_out, 0, buddy, c).start()
 
             return 0
 
@@ -475,17 +475,18 @@
     def lend():
         return remote(recv.at[pl.ds(buddy * owned, owned)], lent, lend_sem.at[0], lend_sem.at[1], at(buddy))
 
-    pass_on(0, held)
-    for c in range(held, chunks):
-        pass_back(c, c + 1)
-        pass_on(c, c + 1)
+    passed = held * HALVES // CHUNKS
+    pass_on(0, passed)
+    for w in range(passed, HALVES * owned):
+        pass_back(w * CHUNKS // HALVES, (w + 1) * CHUNKS // HALVES)
+        pass_on(w, w + 1)
     @pl.when(outer)
     def _():
         await_pots(near_in)
         lend().start()
 
         def arrived(c, _):
-            await_orbit(far_in, c)
+            inner_orbit(c).wait_recv()
             return 0
 
         lax.fori_loop(0, chunks, arrived, 0)
@@ -514,17 +515,17 @@
 
         lax.fori_loop(first, last, step, 0)
 
-    forward_far(0, CHUNKS)
+    forward_far(0, HALVES)
     await_pots(far_in)
     @pl.when(outer)
     def _():
         serve(far_in, 0, owned)
 
-    forward_far(CHUNKS, 2 * CHUNKS)
+    forward_far(HALVES, 2 * HALVES)
     await_pots(far_out)
     serve(far_out, 0, 2)
     for w in range(2, owned):
-        forward_far(CHUNKS * w, CHUNKS * (w + 1))
+        forward_far(HALVES * w, HALVES * (w + 1))
         serve(far_out, w, w + 1)
 
     @pl.when(inner)
@@ -568,14 +569,14 @@
     def _():
         sum_copy(0, at(ahead)).wait_send()
         lend().wait_send()
-        remote(guest.at[0], guest.at[0], orb_send.at[0], orb_recv.at[0, 0], at(ahead)).wait_send()
+        remote(guest.at[0], guest.at[0], orb_send.at[0], orb_recv.at[0], at(ahead)).wait_send()
         through(done.at[pl.ds(0, 2 * owned)], done_sem).wait_send()
 
     @pl.when(inner)
     def _():
         sum_copy(1, at(ahead)).wait_send()
         total_copy().wait_send()
-        remote(guest, guest, orb_send.at[0], orb_recv.at[0, 0], at(ahead)).wait_send()
+        remote(guest, guest, orb_send.at[0], orb_recv.at[0], at(ahead)).wait_send()
         through(done.at[pl.ds(0, 3 * owned)], done_sem).wait_send()
 
     @pl.when(outer)
@@ -641,7 +642,7 @@
                 pltpu.VMEM((line, PLANE, tiles, TILE, nocc), jnp.bfloat16),
                 pltpu.VMEM((owned, PLANE, tiles, TILE, width), jnp.bfloat16),
                 dma((1,)), dma((4,)), dma((2,)), dma((2, 2)), dma((2,)), dma((1,)), dma((planes,)),
-                dma((1,)), dma((planes - 1, CHUNKS * owned)), dma((2,)), dma((2,)),
+                dma((1,)), dma((CHUNKS * owned,)), dma((2, HALVES * owned)), dma((2,)), dma((2,)),
                 pltpu.SemaphoreType.REGULAR, pltpu.SemaphoreType.REGULAR,
             ],
             compiler_params=params,

time: 141 us -> 140 us (level)
  no operation moved by 1% of the time
where the time goes in v10:
time: 140 us; the launch traced here: 139 us
  Pallas kernels  138 us (99%)
    pallas_call x1, Pallas kernels, on_device(): pl.pallas_call(functools.partial(line_kernel, n), out_shape=(pltpu.VMEM(s...  137 us

profile of v10, /device:TPU:0, one launch (start us, length us, event | category | flops | bytes accessed | tf_op | source)
XLA Modules:
  0.0 138.6 jit_solution(7916330510690968593)
XLA Ops:
  0.6 136.6 %shard_map.68 = (bf16[4,16,4,16,256]{4,3,2,1,0:T(8,128)(2,1)S(1)}, f32[4,128]{1,0:T(4,128)S(1)}) custom-call(bf16[128,64,1024]{2,1,0:T(8,128)(2,1)} %chol_hbm.1, bf16[128,64,256]{2,1,0:T(8,128)(2,1)} %half_hbm.1, bf16[64,64,256]{2,1,0:T(8,128)(2,1)} %green_hbm.1, f32[16,4,128]{2,1,0:T(4,128)} %bitcast.4, bf16[4,16,4,16,256]{4,3,2,1,0:T(8,128)(2,1)} %bitcast.3), custom_call_target="tpu_custom_call" | custom-call | tf_op jit(solution)/shard_map/pallas_call | solution.py:623
  137.2 1.4 shard_map.69

commit v11 on v8

--- a/solution.py
+++ b/solution.py
@@ -199,7 +199,7 @@
     chol, half, green, gauss_ref, orb_ref, part, part_in, partial, partial_in, bias_ref, log_all, fields_ref,
     send, recv, guest, done, lent,
     load_sem, aux_sem, part_sem, sum_sem, field_sem, pot_send, pot_recv, orb_send, orb_recv,
-    lend_sem, done_sem, news, ready,
+    lend_sem, done_sem, told,
 ):
     me = lax.axis_index("chol")
     owned = orb_ref.shape[0]
@@ -263,7 +263,7 @@
     def _():
         pl.semaphore_wait(barrier, PLANE)
         for s in others:
-            tell(news, z * PLANE + s)
+            tell(told, z * PLANE + s)
 
     def at(plane):
         return plane * PLANE + seat
@@ -322,8 +322,8 @@
 
     @pl.when(outer)
     def _():
-        pl.semaphore_wait(news, PLANE - 1)
-        tell(ready, at(ahead))
+        pl.semaphore_wait(told, PLANE - 1)
+        tell(told, at(ahead))
 
 
     half_copy.wait()
@@ -349,7 +349,7 @@
 
     @pl.when(inner)
     def _():
-        pl.semaphore_wait(ready, 1)
+        pl.semaphore_wait(told, 1)
 
     def part_copy(there, source):
         return remote(part.at[there], part_in.at[source], part_sem.at[0], part_sem.at[1], z * PLANE + there)
@@ -469,7 +469,7 @@
             push(t, plane)
 
     def lend():
-        return remote(recv.at[pl.ds(buddy * owned, owned)], lent, lend_sem.at[0], lend_sem.at[1], at(buddy))
+        return remote(recv.at[pl.ds(buddy * owned, owned)], lent, lend_sem.at[0], lend_sem.at[0], at(buddy))
 
     pass_back(held, held + 1)
     pass_on(0, held + 1)
@@ -639,8 +639,8 @@
                 pltpu.VMEM((line, PLANE, tiles, TILE, nocc), jnp.bfloat16),
                 pltpu.VMEM((owned, PLANE, tiles, TILE, width), jnp.bfloat16),
                 dma((1,)), dma((4,)), dma((2,)), dma((2, 2)), dma((2,)), dma((1,)), dma((planes,)),
-                dma((1,)), dma((planes - 1, CHUNKS * owned)), dma((2,)), dma((2,)),
-                pltpu.SemaphoreType.REGULAR, pltpu.SemaphoreType.REGULAR,
+                dma((1,)), dma((planes - 1, CHUNKS * owned)), dma((1,)), dma((2,)),
+                pltpu.SemaphoreType.REGULAR,
             ],
             compiler_params=params,
         )(*arrays)

time: 141 us -> 141 us (level)
  no operation moved by 1% of the time
where the time goes in v11:
time: 141 us; the launch traced here: 140 us
  Pallas kernels  140 us (99%)
    pallas_call x1, Pallas kernels, on_device(): pl.pallas_call(functools.partial(line_kernel, n), out_shape=(pltpu.VMEM(s...  138 us

profile of v11, /device:TPU:0, one launch (start us, length us, event | category | flops | bytes accessed | tf_op | source)
XLA Modules:
  0.0 140.5 jit_solution(12705588216718894187)
XLA Ops:
  0.6 138.5 %shard_map.68 = (bf16[4,16,4,16,256]{4,3,2,1,0:T(8,128)(2,1)S(1)}, f32[4,128]{1,0:T(4,128)S(1)}) custom-call(bf16[128,64,1024]{2,1,0:T(8,128)(2,1)} %chol_hbm.1, bf16[128,64,256]{2,1,0:T(8,128)(2,1)} %half_hbm.1, bf16[64,64,256]{2,1,0:T(8,128)(2,1)} %green_hbm.1, f32[16,4,128]{2,1,0:T(4,128)} %bitcast.4, bf16[4,16,4,16,256]{4,3,2,1,0:T(8,128)(2,1)} %bitcast.3), custom_call_target="tpu_custom_call" | custom-call | tf_op jit(solution)/shard_map/pallas_call | solution.py:620
  139.1 1.4 shard_map.69

commit v12 on v8

--- a/solution.py
+++ b/solution.py
@@ -413,8 +413,7 @@
     fields = fields_ref[...].reshape(n * owned, fields_ref.shape[-1])
 
     order = (
-        jnp.where(inner, far_in, near_in), jnp.where(inner, far_out, far_in),
-        jnp.where(inner, near_out, far_out), z,
+        jnp.where(inner, far_in, near_in), far_out, jnp.where(inner, near_out, far_in), z,
     )
 
     def pot_copy(t, plane, there, source):
@@ -512,25 +511,27 @@
 
         lax.fori_loop(first, last, step, 0)
 
-    forward_far(0, CHUNKS)
-    await_pots(far_in)
-    @pl.when(outer)
-    def _():
-        serve(far_in, 0, owned)
-
-    forward_far(CHUNKS, 2 * CHUNKS)
+    forward_far(0, 2 * CHUNKS)
     await_pots(far_out)
     serve(far_out, 0, 2)
     for w in range(2, owned):
         forward_far(CHUNKS * w, CHUNKS * (w + 1))
         serve(far_out, w, w + 1)
 
-    @pl.when(inner)
-    def _():
+        if w == 2:
+            @pl.when(outer)
+            def _():
+                await_pots(far_in)
+                serve(far_in, 0, owned // 2)
+
+    @pl.when(outer)
+    def _():
+        serve(far_in, owned // 2, owned)
+
+    @pl.when(inner)
+    def _():
+        await_pots(far_in)
         serve(far_in, 0, owned)
-
-    @pl.when(inner)
-    def _():
         await_pots(near_out)
         serve(near_out, 0, owned)
 

time: 141 us -> 141 us (level)
  no operation moved by 1% of the time
where the time goes in v12:
time: 141 us
  Pallas kernels  140 us (99%)
    pallas_call x1, Pallas kernels, on_device(): pl.pallas_call(functools.partial(line_kernel, n), out_shape=(pltpu.VMEM(s...  139 us

profile of v12, /device:TPU:0, one launch (start us, length us, event | category | flops | bytes accessed | tf_op | source)
XLA Modules:
  0.0 140.5 jit_solution(10041448853941687606)
XLA Ops:
  0.6 138.5 %shard_map.68 = (bf16[4,16,4,16,256]{4,3,2,1,0:T(8,128)(2,1)S(1)}, f32[4,128]{1,0:T(4,128)S(1)}) custom-call(bf16[128,64,1024]{2,1,0:T(8,128)(2,1)} %chol_hbm.1, bf16[128,64,256]{2,1,0:T(8,128)(2,1)} %half_hbm.1, bf16[64,64,256]{2,1,0:T(8,128)(2,1)} %green_hbm.1, f32[16,4,128]{2,1,0:T(4,128)} %bitcast.4, bf16[4,16,4,16,256]{4,3,2,1,0:T(8,128)(2,1)} %bitcast.3), custom_call_target="tpu_custom_call" | custom-call | tf_op jit(solution)/shard_map/pallas_call | solution.py:621
  139.1 1.4 shard_map.69
